TPU v7x, 256 devices: a whole 4x4x8 slice. The times are simulated.
256 devices in a mesh: dp: 4 (over y), expert: 64 (over x, z, core).
Axes of the slice: x: 4, y: 4, z: 8, core: 2. Of those that a mesh axis runs over, the one named last changes fastest.
Arguments:
- tokens: bfloat16 [32768, 2048], P(('dp', 'expert')), may hold values from -6 to 6
- out_grad: bfloat16 [32768, 2048], P(('dp', 'expert')), may hold values from -6 to 6
- routes: int32 [32768, 6], P(('dp', 'expert')), may hold values from 0 to 63, all different within a row; in each aligned block of 128 rows (0 to 127, 128 to 255, ...) at most 13 rows name the same one
- gate_weights: bfloat16 [32768, 6], P(('dp', 'expert')), may hold values from 0.049804688 to 0.59765625
- saved_preacts: bfloat16 [4, 64, 832, 1408], P('dp', 'expert'), may hold values from -6 to 6
- gate_up: bfloat16 [64, 2048, 1408], P('expert', 'dp'), may hold values from -0.125 to 0.125
- down_proj: bfloat16 [64, 704, 2048], P('expert', 'dp'), may hold values from -0.21875 to 0.21875
Outputs:
- grad_tokens: bfloat16 [32768, 2048], P(('dp', 'expert'))
- grad_gates: bfloat16 [32768, 6], P(('dp', 'expert'))
- grad_gate_up: float32 [64, 2048, 1408], P('expert', 'dp')
- grad_down: float32 [64, 704, 2048], P('expert', 'dp')
Inputs may be any that keep to these rules, and one draw needn't show every extreme that they name: `routes`: each token names 6 different experts. Within the 128 rows of one device no expert is named by more than 13 rows, a bound that some block reaches.
All inputs are finite; a program needn't handle non-finite values.
Results may differ from a plain program's by a relative error of at most 0.0095.
Values may be sent and summed in bfloat16 or wider, within the bound.
A program may use at most 128 MiB of HBM per device.

v0:
```python
import jax
import jax.numpy as jnp
from jax import lax
from jax.sharding import PartitionSpec as P


def in_order(parts, dim):
    shape = list(parts.shape[1:])
    shape[dim] *= parts.shape[0]
    return jnp.moveaxis(parts, 0, dim).reshape(shape)


def work_in_pieces(array, axis, dim, apply, out_dim):
    peers, rows = (lax.axis_size(axis), array.shape[dim])
    count = 2 if rows % 2 == 0 else 1
    gathered, length = ([], rows // count)
    for k in range(count):
        slab = lax.slice_in_dim(array, k * length, (k + 1) * length, axis=dim)
        starts = jnp.arange(peers) * rows + k * length
        gathered.append(jax.vmap(apply)(lax.all_gather(slab, axis), starts))
    return in_order(jnp.concatenate(gathered, axis=out_dim + 1), out_dim)


def find_slots(routes, experts, capacity):
    flat = routes.reshape(-1)
    onehot = (flat[:, None] == jnp.arange(experts, dtype=jnp.int32)[None, :]).astype(jnp.int32)
    before = jnp.cumsum(onehot, axis=0) - onehot
    position = jnp.sum(before * onehot, axis=1)
    return flat * capacity + position


def on_device(tokens, out_grad, routes, gate_weights, saved_preacts, gate_up, down_proj):
    experts = lax.axis_size("expert")
    groups = lax.axis_size("dp")
    tok_rows, top = routes.shape
    width = tokens.shape[1]
    slot_total = saved_preacts.shape[2]
    capacity = slot_total // experts
    hidden = saved_preacts.shape[3] // 2
    slot_index = find_slots(routes, experts, capacity)
    owner_row = jnp.arange(tok_rows * top, dtype=jnp.int32) // top
    send_x = jnp.zeros((slot_total, width), jnp.bfloat16).at[slot_index].set(tokens[owner_row])
    send_dy = jnp.zeros((slot_total, width), jnp.bfloat16).at[slot_index].set(out_grad[owner_row])
    send_g = jnp.zeros((slot_total,), jnp.bfloat16).at[slot_index].set(gate_weights.reshape(-1))
    recv_x, recv_dy, recv_g = (
        lax.all_to_all(
            send_x.reshape(experts, capacity, width),
            "expert",
            split_axis=0,
            concat_axis=0,
            tiled=True,
        ),
        lax.all_to_all(
            send_dy.reshape(experts, capacity, width),
            "expert",
            split_axis=0,
            concat_axis=0,
            tiled=True,
        ),
        lax.all_to_all(
            send_g.reshape(experts, capacity), "expert", split_axis=0, concat_axis=0, tiled=True
        ),
    )
    x_rows = recv_x.reshape(slot_total, width)
    dy_rows = recv_dy.reshape(slot_total, width)
    g_rows = recv_g.reshape(slot_total).astype(jnp.float32)[:, None]
    saved_rows = saved_preacts[0, 0]
    gate_pre = saved_rows[:, :hidden].astype(jnp.float32)
    up_pre = saved_rows[:, hidden:].astype(jnp.float32)
    sigmoid_gate = jax.nn.sigmoid(gate_pre)
    act = (gate_pre * sigmoid_gate * up_pre).astype(jnp.bfloat16)

    def project_down(piece, start):
        return lax.dot_general(
            dy_rows, piece, (((1,), (1,)), ((), ())), preferred_element_type=jnp.float32
        )

    act_grad = work_in_pieces(down_proj[0], "dp", 0, project_down, 1)
    gate_grad_rows = (
        jnp.sum(act.astype(jnp.float32) * act_grad, axis=1) / jnp.sqrt(jnp.float32(width))
    ).astype(jnp.bfloat16)
    scaled_grad = g_rows * act_grad
    grad_gate = scaled_grad * up_pre * sigmoid_gate * (1.0 + gate_pre * (1.0 - sigmoid_gate))
    grad_up = scaled_grad * gate_pre * sigmoid_gate
    pre_grad = jnp.concatenate([grad_gate, grad_up], axis=1).astype(jnp.bfloat16)
    scaled_dy = (g_rows * dy_rows.astype(jnp.float32)).astype(jnp.bfloat16)
    row_grad = lax.dot_general(
        pre_grad,
        lax.all_gather(gate_up[0], "dp", axis=0, tiled=True),
        (((1,), (1,)), ((), ())),
        preferred_element_type=jnp.float32,
    ).astype(jnp.bfloat16)
    back_rows, back_gate = (
        lax.all_to_all(
            row_grad.reshape(experts, capacity, width),
            "expert",
            split_axis=0,
            concat_axis=0,
            tiled=True,
        ),
        lax.all_to_all(
            gate_grad_rows.reshape(experts, capacity),
            "expert",
            split_axis=0,
            concat_axis=0,
            tiled=True,
        ),
    )
    picked = (
        back_rows.reshape(slot_total, width)[slot_index]
        .astype(jnp.float32)
        .reshape(tok_rows, top, width)
    )
    grad_tokens = jnp.sum(picked, axis=1).astype(jnp.bfloat16)
    grad_gates = back_gate.reshape(slot_total)[slot_index].reshape(tok_rows, top)
    grad_scale = 1.0 / jnp.sqrt(jnp.float32(groups * tok_rows * top))
    columns = x_rows
    grad_gu = lax.psum_scatter(
        lax.dot_general(
            columns, pre_grad, (((0,), (0,)), ((), ())), preferred_element_type=jnp.float32
        ).astype(jnp.bfloat16),
        "dp",
        scatter_dimension=0,
        tiled=True,
    ).astype(jnp.float32)
    columns = act
    grad_dn = lax.psum_scatter(
        lax.dot_general(
            columns, scaled_dy, (((0,), (0,)), ((), ())), preferred_element_type=jnp.float32
        ).astype(jnp.bfloat16),
        "dp",
        scatter_dimension=0,
        tiled=True,
    ).astype(jnp.float32)
    return (grad_tokens, grad_gates, (grad_gu * grad_scale)[None], (grad_dn * grad_scale)[None])


def solution(mesh):
    in_specs = (
        P(("dp", "expert"), None),
        P(("dp", "expert"), None),
        P(("dp", "expert"), None),
        P(("dp", "expert"), None),
        P("dp", "expert", None, None),
        P("expert", "dp", None),
        P("expert", "dp", None),
    )
    out_specs = (
        P(("dp", "expert"), None),
        P(("dp", "expert"), None),
        P("expert", "dp", None),
        P("expert", "dp", None),
    )
    return jax.shard_map(
        on_device, mesh=mesh, in_specs=in_specs, out_specs=out_specs, check_vma=False
    )
```

profile of v0, /device:TPU:1, one launch (start us, length us, event | category | flops | bytes accessed | tf_op | source)
XLA Modules:
  0.0 448.4 jit_solution(639122149408087713)
XLA Ops:
  7.2 2.1 fusion.35
  14.7 8.6 %scatter_custom_fusion = bf16[832]{0:T(1024)(128)(2,1)S(1)} fusion(s32[768]{0:T(1024)S(1)} %fusion.28, bf16[768]{0:T(1024)(128)(2,1)S(1)} %reshape.215, bf16[]{:T(256)} %constant.12.clone.1), kind=kCustom, calls=%fused_computation.66 | custom fusion | bytes 1666 | tf_op jit(solution)/shard_map/scatter | solution.py:44
  24.1 13.3 %all-to-all-start = ((bf16[64,1,13]{2,1,0:T(2,128)(2,1)}), bf16[64,1,13]{2,1,0:T(2,128)(2,1)S(1)}, u32[]{:S(2)}, u32[]{:S(2)}) async-start(bf16[64,1,13]{2,1,0:T(2,128)(2,1)} %all_to_all.25), calls=%async_computation | async-start | bytes 65536 | tf_op jit(solution)/shard_map/all_to_all | solution.py:60
  37.4 22.8 %scatter_custom_fusion.1 = bf16[832,2048]{1,0:T(8,128)(2,1)} fusion(s32[768]{0:T(1024)S(1)} %fusion.28, bf16[128,2048]{1,0:T(8,128)(2,1)S(1)} %copy-done, s32[1024]{0:T(1024)S(1)} %pad_clamp_fusion.1, bf16[]{:T(256)} %constant.12.clone.1), kind=kCustom, calls=%fused_computation.23 | custom fusion | bytes 3407874 | tf_op jit(solution)/shard_map/scatter | solution.py:43
  60.2 5.0 %reshape.169 = bf16[64,13,2048]{2,1,0:T(8,128)(2,1)} reshape(bf16[832,2048]{1,0:T(8,128)(2,1)} %scatter_custom_fusion.1) | data formatting | bytes 6815744 | tf_op jit(solution)/shard_map/reshape | solution.py:54
  65.3 10.5 %all-to-all-start.1 = ((bf16[64,13,2048]{2,1,0:T(8,128)(2,1)}), bf16[64,13,2048]{2,1,0:T(8,128)(2,1)}, u32[]{:S(2)}, u32[]{:S(2)}) async-start(bf16[64,13,2048]{2,1,0:T(8,128)(2,1)} %reshape.169), calls=%async_computation.1 | async-start | bytes 8388608 | tf_op jit(solution)/shard_map/all_to_all | solution.py:53
  76.5 29.6 %scatter_custom_fusion.2 = bf16[832,2048]{1,0:T(8,128)(2,1)S(1)} fusion(s32[768]{0:T(1024)S(1)} %fusion.28, bf16[128,2048]{1,0:T(8,128)(2,1)} %param.7, s32[1024]{0:T(1024)S(1)} %pad_clamp_fusion.1, bf16[]{:T(256)} %constant.12.clone.1), kind=kCustom, calls=%fused_computation.21 | custom fusion | bytes 3408384 | tf_op jit(solution)/shard_map/scatter | solution.py:42
  106.0 3.0 reshape.176
  109.0 62.6 %all-to-all-done.1 = bf16[64,13,2048]{2,1,0:T(8,128)(2,1)} async-done(((bf16[64,13,2048]{2,1,0:T(8,128)(2,1)}), bf16[64,13,2048]{2,1,0:T(8,128)(2,1)}, u32[]{:S(2)}, u32[]{:S(2)}) %all-to-all-start.1) | async-done | bytes 3407904 | tf_op jit(solution)/shard_map/all_to_all | solution.py:53
  171.6 5.9 %all-to-all-start.4 = ((bf16[64,13,2048]{2,1,0:T(8,128)(2,1)}), bf16[64,13,2048]{2,1,0:T(8,128)(2,1)}, u32[]{:S(2)}, u32[]{:S(2)}) async-start(bf16[64,13,2048]{2,1,0:T(8,128)(2,1)} %reshape.176), calls=%async_computation.4 | async-start | bytes 8388608 | tf_op jit(solution)/shard_map/all_to_all | solution.py:46
  177.9 3.5 reshape.170
  181.3 7.2 %fusion.7 = bf16[704,2048]{1,0:T(8,128)(2,1)} fusion(bf16[832,2048]{1,0:T(8,128)(2,1)S(1)} %reshape.170, f32[832]{0:T(1024)S(1)} %reshape.178, bf16[832,1408]{1,0:T(8,128)(2,1)} %bitcast.43), kind=kOutput, calls=%fused_computation.18 | convolution fusion | flops 2410381312 | bytes 8850688 | tf_op jit(solution)/shard_map/dot_general | solution.py:128
  188.6 3.5 reshape.236
  192.1 4.1 convolution_bitcast_fusion
  196.2 3.1 convolution_bitcast_fusion.1
  201.0 2.4 copy.27
  203.4 70.1 %all-to-all-done.4 = bf16[64,13,2048]{2,1,0:T(8,128)(2,1)} async-done(((bf16[64,13,2048]{2,1,0:T(8,128)(2,1)}), bf16[64,13,2048]{2,1,0:T(8,128)(2,1)}, u32[]{:S(2)}, u32[]{:S(2)}) %all-to-all-start.4) | async-done | bytes 3407904 | tf_op jit(solution)/shard_map/all_to_all | solution.py:46
  273.5 5.0 %reshape.177 = bf16[832,2048]{1,0:T(8,128)(2,1)} reshape(bf16[64,13,2048]{2,1,0:T(8,128)(2,1)} %all-to-all-done.4) | data formatting | bytes 6815744 | tf_op jit(solution)/shard_map/reshape | solution.py:64
  278.5 4.3 fusion.14
  284.2 8.9 %convolution_convert_fusion = bf16[2048,1408]{1,0:T(8,128)(2,1)} fusion(bf16[832,2048]{1,0:T(8,128)(2,1)S(1)} %copy-done.2, bf16[832,704]{1,0:T(8,128)(2,1)S(1)} %get-tuple-element.13, bf16[832,704]{1,0:T(8,128)(2,1)S(1)} %get-tuple-element.12), kind=kOutput, calls=%fused_computation.7 | convolution fusion | flops 4805853184 | bytes 11517952 | tf_op jit(solution)/shard_map/dot_general | solution.py:119
  293.9 6.1 %all-to-all-start.3 = ((bf16[64,1,13]{2,1,0:T(2,128)(2,1)}), bf16[64,1,13]{2,1,0:T(2,128)(2,1)S(1)}, u32[]{:S(2)}, u32[]{:S(2)}) async-start(bf16[64,1,13]{2,1,0:T(2,128)(2,1)} %convert_element_type.86), calls=%async_computation.3 | async-start | bytes 65536 | tf_op jit(solution)/shard_map/all_to_all | solution.py:101
  300.0 9.4 %fusion.2 = bf16[832,2048]{1,0:T(8,128)(2,1)S(1)} fusion(bf16[1,2048,1408]{2,1,0:T(8,128)(2,1)} %all-gather.9.cloned.1.call-done, bf16[832,704]{1,0:T(8,128)(2,1)} %copy-done.4, bf16[832,704]{1,0:T(8,128)(2,1)} %copy-done.3), kind=kOutput, calls=%fused_computation.15 | convolution fusion | flops 4804673536 | bytes 11517952 | tf_op jit(solution)/shard_map/dot_general | solution.py:87
  309.4 3.0 reshape.172
  312.4 10.5 %all-to-all-start.2 = ((bf16[64,13,2048]{2,1,0:T(8,128)(2,1)}), bf16[64,13,2048]{2,1,0:T(8,128)(2,1)}, u32[]{:S(2)}, u32[]{:S(2)}) async-start(bf16[64,13,2048]{2,1,0:T(8,128)(2,1)} %reshape.172), calls=%async_computation.2 | async-start | bytes 8388608 | tf_op jit(solution)/shard_map/all_to_all | solution.py:94
  323.1 5.0 %gather_fusion.1 = bf16[768]{0:T(1024)(128)(2,1)S(1)} fusion(bf16[832]{0:T(1024)(128)(2,1)S(1)} %reshape.174, s32[1024]{0:T(1024)S(1)} %pad_clamp_fusion), kind=kCustom, calls=%fused_computation.2 | custom fusion | bytes 6144 | tf_op jit(solution)/shard_map/gather | solution.py:115
  329.0 2.4 multiply_bitcast_fusion.1
  331.4 87.4 %all-to-all-done.2 = bf16[64,13,2048]{2,1,0:T(8,128)(2,1)} async-done(((bf16[64,13,2048]{2,1,0:T(8,128)(2,1)}), bf16[64,13,2048]{2,1,0:T(8,128)(2,1)}, u32[]{:S(2)}, u32[]{:S(2)}) %all-to-all-start.2) | async-done | bytes 3407904 | tf_op jit(solution)/shard_map/all_to_all | solution.py:94
  418.8 3.4 reshape.173
  422.2 4.2 gather_fusion
  426.4 6.3 %gather.16 = bf16[128,6,2048]{2,1,0:T(8,128)(2,1)} reshape(bf16[768,2048]{1,0:T(8,128)(2,1)} %gather_fusion) | data formatting | bytes 6291456 | tf_op jit(solution)/shard_map/gather | solution.py:110
  432.7 5.7 %reduce_sum.34 = bf16[128,2048]{1,0:T(8,128)(2,1)} reduce(bf16[128,6,2048]{2,1,0:T(8,128)(2,1)} %gather.16, bf16[]{:T(256)} %constant.12.clone.1), dimensions={1}, to_apply=%region_5.6 | reduce | flops 1310720 | bytes 3670018 | tf_op jit(solution)/shard_map/reduce_sum | solution.py:114
  438.4 3.2 multiply_bitcast_fusion
  (58 shorter events, 12.2 us)
Async XLA Ops:
  7.2 30.2 %copy-start = (bf16[128,2048]{1,0:T(8,128)(2,1)S(1)}, bf16[128,2048]{1,0:T(8,128)(2,1)}, u32[]{:S(2)}) copy-start(bf16[128,2048]{1,0:T(8,128)(2,1)} %param.8) | copy-start | bytes 1572868
  7.2 7.0 %copy-start.6 = (bf16[128,6]{0,1:T(8,128)(2,1)S(1)}, bf16[128,6]{0,1:T(8,128)(2,1)}, u32[]{:S(2)}) copy-start(bf16[128,6]{0,1:T(8,128)(2,1)} %param.10) | copy-start | bytes 4612
  7.2 184.9 %all-gather.7.cloned.1.call-start = ((), (), s32[]{:S(2)}) async-start(), calls=%async_computation.8 | async-start | bytes 1802240 | tf_op jit(solution)/shard_map/all_gather | solution.py:20
  9.3 186.9 %all-gather.5.cloned.1.call-start = ((), (), s32[]{:S(2)}) async-start(), calls=%async_computation.7 | async-start | bytes 1802240 | tf_op jit(solution)/shard_map/all_gather | solution.py:20
  24.1 41.2 %all-to-all-start = ((bf16[64,1,13]{2,1,0:T(2,128)(2,1)}), bf16[64,1,13]{2,1,0:T(2,128)(2,1)S(1)}, u32[]{:S(2)}, u32[]{:S(2)}) async-start(bf16[64,1,13]{2,1,0:T(2,128)(2,1)} %all_to_all.25), calls=%async_computation | async-start | bytes 65536 | tf_op jit(solution)/shard_map/all_to_all | solution.py:60
  65.3 106.4 %all-to-all-start.1 = ((bf16[64,13,2048]{2,1,0:T(8,128)(2,1)}), bf16[64,13,2048]{2,1,0:T(8,128)(2,1)}, u32[]{:S(2)}, u32[]{:S(2)}) async-start(bf16[64,13,2048]{2,1,0:T(8,128)(2,1)} %reshape.169), calls=%async_computation.1 | async-start | bytes 8388608 | tf_op jit(solution)/shard_map/all_to_all | solution.py:53
  75.8 224.3 %all-gather.9.cloned.1.call-start = ((), (), s32[]{:S(2)}) async-start(), calls=%async_computation.11 | async-start | bytes 7208960 | tf_op jit(solution)/shard_map/all_gather | solution.py:89
  171.6 101.8 %all-to-all-start.4 = ((bf16[64,13,2048]{2,1,0:T(8,128)(2,1)}), bf16[64,13,2048]{2,1,0:T(8,128)(2,1)}, u32[]{:S(2)}, u32[]{:S(2)}) async-start(bf16[64,13,2048]{2,1,0:T(8,128)(2,1)} %reshape.176), calls=%async_computation.4 | async-start | bytes 8388608 | tf_op jit(solution)/shard_map/all_to_all | solution.py:46
  177.6 151.4 %reduce-scatter.5.cloned.1.call-start = ((), (), s32[]{:S(2)}) async-start(), calls=%async_computation.10 | async-start | bytes 3604480 | tf_op jit(solution)/shard_map/reduce_scatter | solution.py:127
  188.6 249.9 %reduce-scatter.3.cloned.1.call-start = ((), (), s32[]{:S(2)}) async-start(), calls=%async_computation.9 | async-start | bytes 7208960 | tf_op jit(solution)/shard_map/reduce_scatter | solution.py:118
  196.2 3.2 copy-start.5
  278.5 5.7 %copy-start.2 = (bf16[832,2048]{1,0:T(8,128)(2,1)S(1)}, bf16[832,2048]{1,0:T(8,128)(2,1)}, u32[]{:S(2)}) copy-start(bf16[832,2048]{1,0:T(8,128)(2,1)} %reshape.177) | copy-start | bytes 10223620
  282.7 1.0 copy-start.3
  282.7 1.5 copy-start.4
  293.9 18.5 %all-to-all-start.3 = ((bf16[64,1,13]{2,1,0:T(2,128)(2,1)}), bf16[64,1,13]{2,1,0:T(2,128)(2,1)S(1)}, u32[]{:S(2)}, u32[]{:S(2)}) async-start(bf16[64,1,13]{2,1,0:T(2,128)(2,1)} %convert_element_type.86), calls=%async_computation.3 | async-start | bytes 65536 | tf_op jit(solution)/shard_map/all_to_all | solution.py:101
  312.4 106.4 %all-to-all-start.2 = ((bf16[64,13,2048]{2,1,0:T(8,128)(2,1)}), bf16[64,13,2048]{2,1,0:T(8,128)(2,1)}, u32[]{:S(2)}, u32[]{:S(2)}) async-start(bf16[64,13,2048]{2,1,0:T(8,128)(2,1)} %reshape.172), calls=%async_computation.2 | async-start | bytes 8388608 | tf_op jit(solution)/shard_map/all_to_all | solution.py:94
  432.7 8.9 %copy-start.1 = (bf16[128,2048]{1,0:T(8,128)(2,1)S(1)}, bf16[128,2048]{1,0:T(8,128)(2,1)}, u32[]{:S(2)}) copy-start(bf16[128,2048]{1,0:T(8,128)(2,1)} %param.8) | copy-start | bytes 1572868
Sparse Core Ops, SparseCore 0:
  10.4 31.6 all-gather.6
  44.4 28.5 all-gather.4
  78.4 65.0 all-gather.8
  188.7 39.9 reduce-scatter.4
  293.3 58.9 reduce-scatter.2
where the time goes:
time: 455 us; the launch traced here: 448 us
  waiting for transfers between devices  222 us (49%)
  local copies, waits for them, and re-layouts  113 us (25%)
  starting transfers between devices  46.4 us (10%)
  matrix products  32.7 us (7%)
  other arithmetic  20.1 us (4%)
  between operations  14.3 us (3%)
    all_to_all x1, waiting for transfers between devices, on_device(): lax.all_to_all(row_grad.reshape(experts, capacity, width), 'expert', spli...  87.4 us
    all_to_all x1, waiting for transfers between devices, on_device(): lax.all_to_all(send_x.reshape(experts, capacity, width), 'expert', split_...  70.1 us
    all_to_all x1, waiting for transfers between devices, on_device(): lax.all_to_all(send_dy.reshape(experts, capacity, width), 'expert', split...  62.6 us
    scatter x2, local copies, waits for them, and re-layouts, on_device(): jnp.zeros((slot_total, width), jnp.bfloat16).at[slot_index]  52.4 us
    all_to_all x1, starting transfers between devices, on_device(): lax.all_to_all(send_g.reshape(experts, capacity), 'expert', split_axis=0,...  13.3 us
    all_to_all x1, starting transfers between devices, on_device(): lax.all_to_all(send_dy.reshape(experts, capacity, width), 'expert', split...  10.5 us
    gather x2, local copies, waits for them, and re-layouts, on_device(): back_rows.reshape(slot_total, width)[slot_index].astype(jnp.float32)  10.5 us
    all_to_all x1, starting transfers between devices, on_device(): lax.all_to_all(row_grad.reshape(experts, capacity, width), 'expert', spli...  10.5 us
  transfers between devices with their start and end apart: 10, of which 3 were waited for; matrix products, arithmetic and copies ran while one was open for 35% of the time, Pallas kernels for 0%

commit v1 on v0

v1 whole, which is shorter than its diff:
```python
import functools

import jax
import jax.numpy as jnp
from jax import lax
from jax.experimental import pallas as pl
from jax.experimental.pallas import tpu as pltpu
from jax.sharding import PartitionSpec as P

MESH = pl.DeviceIdType.MESH
BF16, F32 = jnp.bfloat16, jnp.float32
NX, NZ, NC = 4, 8, 2
PEERS = NX * NC
LANES = 128
GATE_LANE = 8


def place():
    e = lax.axis_index("expert")
    return e // (NZ * NC), lax.rem(e // NC, NZ), lax.rem(e, NC)


def device(x, z, c):
    return (lax.axis_index("dp"), (x * NZ + z) * NC + c)


def enter(x, z, c):
    barrier = pltpu.get_barrier_semaphore()
    for step in (1, NZ - 1):
        pl.semaphore_signal(barrier, inc=1, device_id=device(x, lax.rem(z + step, NZ), c), device_id_type=MESH)
    me = x * NC + c
    for step in range(1, PEERS):
        peer = lax.rem(me + step, PEERS)
        pl.semaphore_signal(barrier, inc=1, device_id=device(peer // NC, z, lax.rem(peer, NC)), device_id_type=MESH)
    pl.semaphore_wait(barrier, 2 + PEERS - 1)


def chunks_of(widths, first):
    out, spans = [], first
    for group, ws in enumerate(widths):
        col = 0
        for n, w in enumerate(ws):
            segments, off = [], 0
            for array, extra in spans[group] if n == 0 else ():
                segments.append((array, 0, extra, 0))
                off = extra
            segments.append((first["main"][group], col, w, off))
            col += w
            out.append((segments, off + w))
    return out


def dispatch_kernel(chunks, cap, side_ref, dy_ref, x_ref, side_out, dy_out, x_out, gathered_out, *scratch):
    n = len(chunks)
    ring, stage = scratch[:n], scratch[n : 2 * n]
    pick, z_send, z_recv, x_send, x_recv, own_sem, out_sem = scratch[2 * n :]
    ins, outs = (side_ref, dy_ref, x_ref), (side_out, dy_out, x_out)
    x, z, c = place()
    me = x * NC + c
    tok = dy_ref.shape[0]
    half_rows = tok // 2
    block = pick.shape[1]
    sends = NZ - 1

    for (segments, _), buf in zip(chunks, ring):
        for array, col, w, off in segments:
            buf[z, :, off : off + w] = ins[array][:, col : col + w]
    enter(x, z, c)

    def hop(ch, way, i):
        step = 1 if way == 0 else NZ - 1
        dist = i // 2
        half = lax.rem(i + way, 2)
        blk = lax.rem(z + (NZ - step) * dist, NZ)
        view = ring[ch].at[blk, pl.ds(pl.multiple_of(half * half_rows, half_rows), half_rows), :]
        return pltpu.make_async_remote_copy(
            src_ref=view,
            dst_ref=view,
            send_sem=z_send.at[ch, way, i],
            recv_sem=z_recv.at[ch, way, i],
            device_id=device(x, lax.rem(z + step, NZ), c),
            device_id_type=MESH,
        )

    def z_start(ch, i):
        for way in (0, 1):
            hop(ch, way, i).start()

    def z_arrived(ch, i):
        for way in (0, 1):
            hop(ch, way, i).wait_recv()

    def x_copies(ch, peer, slot, own):
        segments, _ = chunks[ch]
        made = []
        for array, col, w, off in segments:
            src = stage[ch].at[peer, :, off : off + w]
            dst = outs[array].at[slot, :, col : col + w]
            sem = (ch, slot if own is None else own, 0 if array == 0 else 1)
            made.append((src, dst, array))
        return made

    def x_send_copy(ch, peer):
        out = []
        for src, dst, array in x_copies(ch, peer, me, None):
            kind = 0 if array == 0 else 1
            out.append(
                pltpu.make_async_remote_copy(
                    src_ref=src,
                    dst_ref=dst,
                    send_sem=x_send.at[ch, kind, peer],
                    recv_sem=x_recv.at[ch, kind, me],
                    device_id=device(peer // NC, z, lax.rem(peer, NC)),
                    device_id_type=MESH,
                )
            )
        return out

    def x_recv_copy(ch, peer):
        out = []
        for src, dst, array in x_copies(ch, peer, peer, None):
            kind = 0 if array == 0 else 1
            out.append(
                pltpu.make_async_remote_copy(
                    src_ref=src,
                    dst_ref=dst,
                    send_sem=x_send.at[ch, kind, peer],
                    recv_sem=x_recv.at[ch, kind, peer],
                    device_id=device(peer // NC, z, lax.rem(peer, NC)),
                    device_id_type=MESH,
                )
            )
        return out

    def own_copy(ch):
        return [
            pltpu.make_async_copy(src, dst, own_sem.at[ch, 0 if array == 0 else 1])
            for src, dst, array in x_copies(ch, me, me, None)
        ]

    def make_pick():
        lane = lax.broadcasted_iota(jnp.int32, (LANES, tok), 0)
        eye = (lax.broadcasted_iota(jnp.int32, (LANES, LANES), 0) == lax.broadcasted_iota(jnp.int32, (LANES, LANES), 1)).astype(BF16)
        earlier = (
            lax.broadcasted_iota(jnp.int32, (tok, tok), 0) < lax.broadcasted_iota(jnp.int32, (tok, tok), 1)
        ).astype(BF16)
        slot_row = lax.broadcasted_iota(jnp.int32, (block, tok), 0).astype(F32)
        peer_row = lax.broadcasted_iota(jnp.int32, (PEERS, tok), 0)
        expert_row = ((peer_row // NC) * (NZ * NC) + z * NC + lax.rem(peer_row, NC)).astype(F32)
        del lane

        def one(s, _):
            side = ring[0][s, :, 0:LANES]
            turned = lax.dot_general(eye, side, (((1,), (1,)), ((), ())), preferred_element_type=F32)
            match = jnp.zeros((PEERS, tok), F32)
            for k in range(6):
                match = match + (jnp.broadcast_to(turned[k : k + 1, :], (PEERS, tok)) == expert_row).astype(F32)
            position = jnp.dot(match.astype(BF16), earlier, preferred_element_type=F32)
            slot = jnp.where(match > 0.0, position + (s * cap).astype(F32), -1.0)
            for peer in range(PEERS):
                hit = jnp.broadcast_to(slot[peer : peer + 1, :], (block, tok)) == slot_row
                pick[peer, :, pl.ds(pl.multiple_of(s * tok, tok), tok)] = hit.astype(F32).astype(BF16)
            return 0

        lax.fori_loop(0, NZ, one, 0)

    def piece(ch, peer):
        width = chunks[ch][1]
        rows = pick[peer]
        for lo in range(0, width, 256):
            w = min(256, width - lo)
            cols = ring[ch][:, :, lo : lo + w].reshape(NZ * tok, w)
            stage[ch][peer, :, lo : lo + w] = jnp.dot(rows, cols, preferred_element_type=F32).astype(BF16)

        @pl.when(peer != me)
        def _():
            for copy in x_send_copy(ch, peer):
                copy.start()

        @pl.when(peer == me)
        def _():
            for copy in own_copy(ch):
                copy.start()

    def pieces(ch, lo, hi):
        def one(peer, _):
            piece(ch, peer)
            return 0

        lax.fori_loop(lo, hi, one, 0)

    ticks = sends - 2
    for ch in range(n):
        z_start(ch, 0)
        z_start(ch, 1)
        if ch > 0:
            z_arrived(ch - 1, sends - 2)
            z_arrived(ch - 1, sends - 1)
            if ch == 1:
                make_pick()

        def tick(i, _, ch=ch):
            z_arrived(ch, i)
            z_start(ch, i + 2)
            if ch > 0:
                pieces(ch - 1, (PEERS * i) // ticks, (PEERS * (i + 1)) // ticks)
            return 0

        lax.fori_loop(0, ticks, tick, 0)
    z_arrived(n - 1, sends - 2)
    z_arrived(n - 1, sends - 1)
    if n == 1:
        make_pick()
    pieces(n - 1, 0, PEERS)
    keep = pltpu.make_async_copy(ring[0].at[:, :, 0:LANES], gathered_out, out_sem)
    keep.start()
    for ch in range(n):

        def finish(i, _, ch=ch):
            for way in (0, 1):
                hop(ch, way, i).wait_send()
            return 0

        lax.fori_loop(0, sends, finish, 0)

        def arrive(step, _, ch=ch):
            peer = lax.rem(me + step, PEERS)
            for copy in x_recv_copy(ch, peer):
                copy.wait_recv()
            for copy in x_send_copy(ch, peer):
                copy.wait_send()
            return 0

        lax.fori_loop(1, PEERS, arrive, 0)
        for copy in own_copy(ch):
            copy.wait()
    keep.wait()


def dispatch(side, dy, x, cap):
    tok, width = dy.shape
    block = NZ * cap
    parts = {0: [(0, LANES)], 1: [], "main": (1, 2)}
    chunks = chunks_of(([width // 2] * 2, [width // 2] * 2), parts)
    n = len(chunks)
    vmem = pl.BlockSpec(memory_space=pltpu.VMEM)
    anywhere = pl.BlockSpec(memory_space=pl.ANY)
    return pl.pallas_call(
        functools.partial(dispatch_kernel, chunks, cap),
        out_shape=(
            jax.ShapeDtypeStruct((PEERS, block, LANES), BF16),
            jax.ShapeDtypeStruct((PEERS, block, width), BF16),
            jax.ShapeDtypeStruct((PEERS, block, width), BF16),
            jax.ShapeDtypeStruct((NZ, tok, LANES), BF16),
        ),
        in_specs=[vmem] * 3,
        out_specs=(anywhere,) * 4,
        scratch_shapes=[pltpu.VMEM((NZ, tok, w), BF16) for _, w in chunks]
        + [pltpu.VMEM((PEERS, block, w), BF16) for _, w in chunks]
        + [
            pltpu.VMEM((PEERS, block, NZ * tok), BF16),
            pltpu.SemaphoreType.DMA((n, 2, NZ - 1)),
            pltpu.SemaphoreType.DMA((n, 2, NZ - 1)),
            pltpu.SemaphoreType.DMA((n, 2, PEERS)),
            pltpu.SemaphoreType.DMA((n, 2, PEERS)),
            pltpu.SemaphoreType.DMA((n, 2)),
            pltpu.SemaphoreType.DMA,
        ],
        compiler_params=pltpu.CompilerParams(collective_id=0, has_side_effects=True, vmem_limit_bytes=48 << 20),
        cost_estimate=pl.CostEstimate(flops=8_000_000_000, bytes_accessed=250_000_000, transcendentals=0),
        name="dispatch",
    )(side, dy, x)


def give_back_kernel(chunks, cap, side_ref, gate_ref, row_ref, gate_out, tok_out, *scratch):
    n = len(chunks)
    landed, total, leave, come = (scratch[k * n : (k + 1) * n] for k in range(4))
    spread, z_send, z_recv, x_send, x_recv, own_sem = scratch[4 * n :]
    ins, outs = (gate_ref, row_ref), (gate_out, tok_out)
    x, z, c = place()
    me = x * NC + c
    tok = tok_out.shape[0]
    half_rows = tok // 2
    block = row_ref.shape[1]
    pad = landed[0].shape[1]
    sends = NZ - 1

    for buf, (_, w) in zip(landed, chunks):
        buf[:, block:, :] = jnp.zeros((PEERS, pad - block, w), BF16)
    enter(x, z, c)

    def x_copies(ch, src_slot, dst_slot, sem_slot, peer):
        made = []
        for array, col, w, off in chunks[ch][0]:
            made.append(
                pltpu.make_async_remote_copy(
                    src_ref=ins[array].at[src_slot, :, col : col + w],
                    dst_ref=landed[ch].at[dst_slot, 0:block, off : off + w],
                    send_sem=x_send.at[ch, array, peer],
                    recv_sem=x_recv.at[ch, array, sem_slot],
                    device_id=device(peer // NC, z, lax.rem(peer, NC)),
                    device_id_type=MESH,
                )
            )
        return made

    def own_copy(ch):
        return [
            pltpu.make_async_copy(
                ins[array].at[me, :, col : col + w], landed[ch].at[me, 0:block, off : off + w], own_sem.at[ch, array]
            )
            for array, col, w, off in chunks[ch][0]
        ]

    for ch in range(n):

        def send(step, _, ch=ch):
            peer = lax.rem(me + step, PEERS)
            for copy in x_copies(ch, peer, me, me, peer):
                copy.start()
            return 0

        lax.fori_loop(1, PEERS, send, 0)
        for copy in own_copy(ch):
            copy.start()

    later = (
        lax.broadcasted_iota(jnp.int32, (tok, tok), 1) < lax.broadcasted_iota(jnp.int32, (tok, tok), 0)
    ).astype(BF16)
    lane = lax.broadcasted_iota(jnp.int32, (tok, LANES), 1)
    expert_lane = jnp.where(lane < PEERS, (lane // NC) * (NZ * NC) + z * NC + lax.rem(lane, NC), -1).astype(F32)
    slot_lane = lax.broadcasted_iota(jnp.int32, (tok, pad), 1).astype(F32)

    def spread_one(s, _):
        side = side_ref[s].astype(F32)
        match = jnp.zeros((tok, LANES), F32)
        for k in range(6):
            match = match + (jnp.broadcast_to(side[:, k : k + 1], (tok, LANES)) == expert_lane).astype(F32)
        position = jnp.dot(later, match.astype(BF16), preferred_element_type=F32)
        slot = jnp.where(match > 0.0, position + (s * cap).astype(F32), -1.0)
        for peer in range(PEERS):
            hit = jnp.broadcast_to(slot[:, peer : peer + 1], (tok, pad)) == slot_lane
            spread[s, :, peer * pad : (peer + 1) * pad] = hit.astype(F32).astype(BF16)
        return 0

    lax.fori_loop(0, NZ, spread_one, 0)

    def x_arrived(ch):
        def one(step, _):
            peer = lax.rem(me + step, PEERS)
            for copy in x_copies(ch, peer, peer, peer, peer):
                copy.wait_recv()
            return 0

        lax.fori_loop(1, PEERS, one, 0)
        for copy in own_copy(ch):
            copy.wait()

    def combine(ch, k):
        width = chunks[ch][1]
        s = lax.rem(z + NZ // 2 + k, NZ)
        rows = spread[s]
        for lo in range(0, width, 256):
            w = min(256, width - lo)
            cols = landed[ch][:, :, lo : lo + w].reshape(PEERS * pad, w)
            total[ch][s, :, lo : lo + w] = jnp.dot(rows, cols, preferred_element_type=F32)

    def combines(ch, lo, hi):
        def one(k, _):
            combine(ch, k)
            return 0

        lax.fori_loop(lo, hi, one, 0)

    def hop(ch, way, i):
        step = 1 if way == 0 else NZ - 1
        return pltpu.make_async_remote_copy(
            src_ref=leave[ch].at[way, i],
            dst_ref=come[ch].at[way, i],
            send_sem=z_send.at[ch, way, i],
            recv_sem=z_recv.at[ch, way, i],
            device_id=device(x, lax.rem(z + step, NZ), c),
            device_id_type=MESH,
        )

    def part(ch, way, i):
        step = 1 if way == 0 else NZ - 1
        dist = NZ // 2 - (i + 1) // 2
        half = lax.rem(i + way, 2)
        s = lax.rem(z + step * dist, NZ)
        return total[ch][s, pl.ds(pl.multiple_of(half * half_rows, half_rows), half_rows), :]

    def z_step(ch, i, first):
        for way in (0, 1):
            value = part(ch, way, i)
            if not first:
                hop(ch, way, i - 2).wait_recv()
                value = value + come[ch][way, i - 2].astype(F32)
            leave[ch][way, i] = value.astype(BF16)
            hop(ch, way, i).start()

    def finish(ch):
        for way in (0, 1):
            hop(ch, way, sends - 2).wait_recv()
            hop(ch, way, sends - 1).wait_recv()
        for half in (0, 1):
            rows = slice(half * half_rows, (half + 1) * half_rows)
            value = total[ch][z, rows, :]
            for way in (0, 1):
                i = sends - 1 if (sends - 1 + way) % 2 == half else sends - 2
                value = value + come[ch][way, i].astype(F32)
            for array, col, w, off in chunks[ch][0]:
                outs[array][rows, col : col + w] = value[:, off : off + w].astype(BF16)

    x_arrived(0)
    combines(0, 0, NZ)
    ticks = sends - 2
    for ch in range(n):
        z_step(ch, 0, True)
        z_step(ch, 1, True)
        if ch > 0:
            finish(ch - 1)
        if ch + 1 < n:
            x_arrived(ch + 1)

        def tick(i, _, ch=ch):
            z_step(ch, i + 2, False)
            if ch + 1 < n:
                combines(ch + 1, (NZ * i) // ticks, (NZ * (i + 1)) // ticks)
            return 0

        lax.fori_loop(0, ticks, tick, 0)
    finish(n - 1)
    for ch in range(n):

        def drain(i, _, ch=ch):
            for way in (0, 1):
                hop(ch, way, i).wait_send()
            return 0

        lax.fori_loop(0, sends, drain, 0)

        def sent(step, _, ch=ch):
            peer = lax.rem(me + step, PEERS)
            for copy in x_copies(ch, peer, me, me, peer):
                copy.wait_send()
            return 0

        lax.fori_loop(1, PEERS, sent, 0)


def give_back(side, gate_rows, rows, cap):
    block, width = rows.shape[1:]
    tok = side.shape[1]
    pad = -(-block // LANES) * LANES
    parts = {0: [(0, LANES)], "main": (1,)}
    chunks = chunks_of(([width // 4] * 4,), parts)
    n = len(chunks)
    vmem = pl.BlockSpec(memory_space=pltpu.VMEM)
    return pl.pallas_call(
        functools.partial(give_back_kernel, chunks, cap),
        out_shape=(jax.ShapeDtypeStruct((tok, LANES), BF16), jax.ShapeDtypeStruct((tok, width), BF16)),
        in_specs=[vmem, vmem, vmem],
        out_specs=(vmem, vmem),
        scratch_shapes=[pltpu.VMEM((PEERS, pad, w), BF16) for _, w in chunks]
        + [pltpu.VMEM((NZ, tok, w), F32) for _, w in chunks]
        + [pltpu.VMEM((2, NZ - 1, tok // 2, w), BF16) for _, w in chunks] * 2
        + [
            pltpu.VMEM((NZ, tok, PEERS * pad), BF16),
            pltpu.SemaphoreType.DMA((n, 2, NZ - 1)),
            pltpu.SemaphoreType.DMA((n, 2, NZ - 1)),
            pltpu.SemaphoreType.DMA((n, 2, PEERS)),
            pltpu.SemaphoreType.DMA((n, 2, PEERS)),
            pltpu.SemaphoreType.DMA((n, 2)),
        ],
        compiler_params=pltpu.CompilerParams(collective_id=1, has_side_effects=True, vmem_limit_bytes=48 << 20),
        cost_estimate=pl.CostEstimate(flops=5_000_000_000, bytes_accessed=170_000_000, transcendentals=0),
        name="give_back",
    )(side, gate_rows, rows)


def on_device(tokens, out_grad, routes, gate_weights, saved_preacts, gate_up, down_proj):
    experts = lax.axis_size("expert")
    groups = lax.axis_size("dp")
    tok_rows, top = routes.shape
    width = tokens.shape[1]
    slot_total = saved_preacts.shape[2]
    cap = slot_total // experts
    hidden = saved_preacts.shape[3] // 2
    lane = lax.broadcasted_iota(jnp.int32, (tok_rows, LANES), 1)
    side = jnp.zeros((tok_rows, LANES), BF16)
    for k in range(top):
        side = jnp.where(lane == k, routes[:, k : k + 1].astype(BF16), side)
        side = jnp.where(lane == GATE_LANE + k, gate_weights[:, k : k + 1], side)
    down = lax.all_gather(down_proj[0], "dp", axis=0, tiled=True)
    up = lax.all_gather(gate_up[0], "dp", axis=0, tiled=True)
    side_rows, dy_rows, x_rows, sides = dispatch(side, out_grad, tokens, cap)

    per_x = NZ * NC * cap
    new = lax.broadcasted_iota(jnp.int32, (per_x, per_x), 0)
    old = lax.broadcasted_iota(jnp.int32, (per_x, per_x), 1)
    core, zed, p = new // (NZ * cap), (new // cap) % NZ, new % cap
    order = (old == (zed * NC + core) * cap + p).astype(BF16)
    saved_rows = (
        jnp.einsum("ij,xjf->xif", order, saved_preacts[0, 0].reshape(NX, per_x, 2 * hidden), preferred_element_type=F32)
        .astype(BF16)
        .reshape(slot_total, 2 * hidden)
    )
    side_rows = side_rows.reshape(slot_total, LANES)
    dy_rows = dy_rows.reshape(slot_total, width)
    x_rows = x_rows.reshape(slot_total, width)
    mine = side_rows[:, :top] == lax.axis_index("expert").astype(BF16)
    g_rows = jnp.sum(
        jnp.where(mine, side_rows[:, GATE_LANE : GATE_LANE + top], 0).astype(F32), axis=1, keepdims=True
    )
    gate_pre = saved_rows[:, :hidden].astype(F32)
    up_pre = saved_rows[:, hidden:].astype(F32)
    sigmoid_gate = jax.nn.sigmoid(gate_pre)
    act = (gate_pre * sigmoid_gate * up_pre).astype(BF16)
    act_grad = lax.dot_general(dy_rows, down, (((1,), (1,)), ((), ())), preferred_element_type=F32)
    gate_grad_rows = (jnp.sum(act.astype(F32) * act_grad, axis=1, keepdims=True) / jnp.sqrt(F32(width))).astype(BF16)
    scaled_grad = g_rows * act_grad
    grad_gate = scaled_grad * up_pre * sigmoid_gate * (1.0 + gate_pre * (1.0 - sigmoid_gate))
    grad_up = scaled_grad * gate_pre * sigmoid_gate
    pre_grad = jnp.concatenate([grad_gate, grad_up], axis=1).astype(BF16)
    scaled_dy = (g_rows * dy_rows.astype(F32)).astype(BF16)
    row_grad = lax.dot_general(pre_grad, up, (((1,), (1,)), ((), ())), preferred_element_type=F32).astype(BF16)
    row_lane = lax.broadcasted_iota(jnp.int32, (slot_total, LANES), 1)
    own = (row_lane < top) & (side_rows == lax.axis_index("expert").astype(BF16))
    gate_back = jnp.where(own, gate_grad_rows, 0).astype(BF16)
    gates, grad_tokens = give_back(
        sides, gate_back.reshape(PEERS, -1, LANES), row_grad.reshape(PEERS, -1, width), cap
    )
    grad_scale = 1.0 / jnp.sqrt(F32(groups * tok_rows * top))
    grad_gu = lax.psum_scatter(
        lax.dot_general(x_rows, pre_grad, (((0,), (0,)), ((), ())), preferred_element_type=F32).astype(BF16),
        "dp",
        scatter_dimension=0,
        tiled=True,
    ).astype(F32)
    grad_dn = lax.psum_scatter(
        lax.dot_general(act, scaled_dy, (((0,), (0,)), ((), ())), preferred_element_type=F32).astype(BF16),
        "dp",
        scatter_dimension=0,
        tiled=True,
    ).astype(F32)
    return (grad_tokens, gates[:, :top], (grad_gu * grad_scale)[None], (grad_dn * grad_scale)[None])


def solution(mesh):
    in_specs = (
        P(("dp", "expert"), None),
        P(("dp", "expert"), None),
        P(("dp", "expert"), None),
        P(("dp", "expert"), None),
        P("dp", "expert", None, None),
        P("expert", "dp", None),
        P("expert", "dp", None),
    )
    out_specs = (
        P(("dp", "expert"), None),
        P(("dp", "expert"), None),
        P("expert", "dp", None),
        P("expert", "dp", None),
    )
    return jax.shard_map(
        on_device, mesh=mesh, in_specs=in_specs, out_specs=out_specs, check_vma=False
    )
```

time: 455 us -> 351 us (0.77); the launches traced: 448 us -> 351 us
  Pallas kernels: 0 us -> 203 us
  waiting for transfers between devices: 222 us -> 82.6 us
  local copies, waits for them, and re-layouts: 113 us -> 12.6 us
  starting transfers between devices: 46.4 us -> 0.16 us
  other arithmetic: 20.1 us -> 7.04 us
    all_to_all x5 -> x0, waiting for transfers between devices: 220 us -> none  [the longest x1 87.4 us: on_device(): lax.all_to_all(row_grad.reshape(experts, capacity, width), 'expert', spli...]
    pallas_call x0 -> x2, Pallas kernels: none -> 203 us  [the longest x1 125 us: dispatch(): pl.pallas_call(functools.partial(dispatch_kernel, chunks, cap), out_shape...]
    all_gather x3 -> x2, waiting for transfers between devices: 0.04 us -> 63 us  [the longest x1 63 us: on_device(): up = lax.all_gather(gate_up[0], 'dp', axis=0, tiled=True)]
    scatter x3 -> x0, local copies, waits for them, and re-layouts: 61 us -> none  [the longest x2 52.4 us: on_device(): jnp.zeros((slot_total, width), jnp.bfloat16).at[slot_index]]
    all_to_all x5 -> x0, starting transfers between devices: 46.2 us -> none  [the longest x1 13.3 us: on_device(): lax.all_to_all(send_g.reshape(experts, capacity), 'expert', split_axis=0,...]
    reshape x11 -> x0, local copies, waits for them, and re-layouts: 29.2 us -> none  [the longest x2 6.9 us: on_device(): dy_rows = recv_dy.reshape(slot_total, width)]
    reduce_scatter x2, waiting for transfers between devices: 0.01 us -> 18.2 us  [the longest x1 18.2 us: on_device(): lax.psum_scatter(lax.dot_general(act, scaled_dy, (((0,), (0,)), ((), ()))...]
    gather x3 -> x0, local copies, waits for them, and re-layouts: 15.5 us -> none  [the longest x2 10.5 us: on_device(): back_rows.reshape(slot_total, width)[slot_index].astype(jnp.float32)]
  transfers between devices with their start and end apart: 10 -> 4, of which waited for: 3 -> 2; matrix products, arithmetic and copies ran while one was open for 35% -> 12% of each run, Pallas kernels for 0% -> 58%
where the time goes in v1:
time: 351 us
  Pallas kernels  203 us (58%)
  waiting for transfers between devices  82.6 us (24%)
  matrix products  31.7 us (9%)
  between operations  14 us (4%)
  local copies, waits for them, and re-layouts  12.6 us (4%)
  other arithmetic  7.04 us (2%)
    pallas_call x1, Pallas kernels, dispatch(): pl.pallas_call(functools.partial(dispatch_kernel, chunks, cap), out_shape...  125 us
    pallas_call x1, Pallas kernels, give_back(): pl.pallas_call(functools.partial(give_back_kernel, chunks, cap), out_shap...  77.5 us
    all_gather x1, waiting for transfers between devices, on_device(): up = lax.all_gather(gate_up[0], 'dp', axis=0, tiled=True)  63 us
    reduce_scatter x1, waiting for transfers between devices, on_device(): lax.psum_scatter(lax.dot_general(act, scaled_dy, (((0,), (0,)), ((), ()))...  18.2 us
    unnamed x24, local copies, waits for them, and re-layouts  10.5 us
    dot_general x1, matrix products, on_device(): lax.dot_general(pre_grad, up, (((1,), (1,)), ((), ())), preferred_element...  8.69 us
    dot_general x1, matrix products, on_device(): lax.dot_general(x_rows, pre_grad, (((0,), (0,)), ((), ())), preferred_ele...  8.52 us
    dot_general x1, matrix products, on_device(): lax.dot_general(dy_rows, down, (((1,), (1,)), ((), ())), preferred_elemen...  8.08 us
  transfers between devices with their start and end apart: 4, of which 2 were waited for; matrix products, arithmetic and copies ran while one was open for 12% of the time, Pallas kernels for 58%

profile of v1, /device:TPU:1, one launch (start us, length us, event | category | flops | bytes accessed | tf_op | source)
XLA Modules:
  0.0 350.7 jit_solution(3142059469368793692)
XLA Ops:
  7.2 0.0 all-gather.5.cloned.1.call-start
  7.2 0.7 all-gather.5.cloned.1.call-update
  7.9 0.0 reduce-scatter.5.cloned.1.call-start
  8.0 0.7 convert.14
  8.7 0.1 copy-done
  8.8 1.4 convolution_convert_fusion.1
  10.2 2.0 fusion.56
  12.3 2.5 copy.14
  14.8 2.5 copy.15
  17.3 0.3 select_select_fusion.1.side_ref
  17.6 1.0 copy-done.2
  18.6 125.0 %dispatch.1 = (bf16[8,104,128]{2,1,0:T(8,128)(2,1)S(1)}, bf16[8,104,2048]{2,1,0:T(8,128)(2,1)S(1)}, bf16[8,104,2048]{2,1,0:T(8,128)(2,1)}, bf16[8,128,128]{2,1,0:T(8,128)(2,1)S(1)}) custom-call(bf16[128,128]{1,0:T(8,128)(2,1)S(1)} %select_select_fusion.1.side_ref, bf16[128,2048]{1,0:T(8,128)(2,1)S(1)} %copy-done.1, bf16[128,2048]{1,0:T(8,128)(2,1)S(1)} %copy-done.2), custom_call_target="tpu_custom_call" | custom-call | flops 8000000000 | bytes 250000000 | tf_op jit(solution)/shard_map/dispatch/pallas_call | solution.py:248
  143.7 0.3 convert_reduce_fusion
  143.9 1.5 copy-done.3
  145.4 5.1 %fusion.7 = bf16[704,2048]{1,0:T(8,128)(2,1)} fusion(bf16[832,2048]{1,0:T(8,128)(2,1)S(1)} %bitcast.56, f32[832]{0:T(1024)S(1)} %convert_reduce_fusion, bf16[832,704]{0,1:T(8,128)(2,1)S(1)} %copy-done.5, bf16[832,704]{0,1:T(8,128)(2,1)S(1)} %copy-done.4), kind=kOutput, calls=%fused_computation.12 | convolution fusion | flops 2410381312 | bytes 8637696 | tf_op jit(solution)/shard_map/dot_general | solution.py:542
  150.5 0.0 all-gather.7.cloned.1.call-start
  150.6 0.7 all-gather.7.cloned.1.call-update
  151.2 0.0 reduce-scatter.3.cloned.1.call-start
  151.3 8.1 %fusion.13 = (bf16[832,704]{0,1:T(8,128)(2,1)S(1)}, f32[832]{0:T(1024)S(1)}, bf16[832,704]{0,1:T(8,128)(2,1)S(1)}) fusion(bf16[832,704]{0,1:T(8,128)(2,1)} %copy.15, bf16[832,704]{0,1:T(8,128)(2,1)} %copy.14, f32[832]{0:T(1024)S(1)} %convert_reduce_fusion, bf16[832,2048]{1,0:T(8,128)(2,1)} %bitcast.57, bf16[1,704,2048]{2,1,0:T(8,128)(2,1)} %all-gather.5.cloned.1.call-done), kind=kOutput, calls=%fused_computation.21 | convolution fusion | flops 2412027136 | bytes 10983936 | tf_op jit(solution)/shard_map/dot_general | solution.py:520
  159.4 1.0 copy-done.8
  160.5 0.4 copy-done.9
  160.9 8.5 %convolution_convert_fusion = bf16[2048,1408]{1,0:T(8,128)(2,1)} fusion(bf16[832,2048]{1,0:T(8,128)(2,1)S(1)} %bitcast.60, bf16[832,704]{0,1:T(8,128)(2,1)S(1)} %get-tuple-element.22, bf16[832,704]{0,1:T(8,128)(2,1)S(1)} %get-tuple-element.20), kind=kOutput, calls=%fused_computation | convolution fusion | flops 4805853184 | bytes 11517952 | tf_op jit(solution)/shard_map/dot_general | solution.py:536
  169.4 0.1 convert_element_type.77
  169.5 0.2 and_select_fusion.gate_ref
  169.7 18.2 %reduce-scatter.5.cloned.1.call-done = bf16[176,2048]{1,0:T(8,128)(2,1)} async-done(((bf16[704,2048]{1,0:T(8,128)(2,1)}), bf16[176,2048]{1,0:T(8,128)(2,1)}) %reduce-scatter.5.cloned.1.call-update) | async-done | bytes 720912 | tf_op jit(solution)/shard_map/reduce_scatter | solution.py:541
  187.9 2.4 multiply_bitcast_fusion.1
  190.3 63.0 %all-gather.7.cloned.1.call-done = bf16[1,2048,1408]{2,1,0:T(8,128)(2,1)} async-done(((bf16[1,512,1408]{2,1,0:T(8,128)(2,1)}), bf16[1,2048,1408]{2,1,0:T(8,128)(2,1)}) %all-gather.7.cloned.1.call-update) | async-done | bytes 5767184 | tf_op jit(solution)/shard_map/all_gather | solution.py:496
  253.3 8.7 %fusion.2 = bf16[832,2048]{1,0:T(8,128)(2,1)S(1)} fusion(bf16[1,2048,1408]{2,1,0:T(8,128)(2,1)} %all-gather.7.cloned.1.call-done, bf16[832,704]{0,1:T(8,128)(2,1)} %copy-done.9, bf16[832,704]{0,1:T(8,128)(2,1)} %copy-done.8), kind=kOutput, calls=%fused_computation.9 | convolution fusion | flops 4804673536 | bytes 11517952 | tf_op jit(solution)/shard_map/dot_general | solution.py:527
  262.0 77.5 %give_back.1 = (bf16[128,128]{1,0:T(8,128)(2,1)S(1)}, bf16[128,2048]{1,0:T(8,128)(2,1)S(1)}) custom-call(bf16[8,128,128]{2,1,0:T(8,128)(2,1)S(1)} %get-tuple-element.10.side_ref, bf16[8,104,128]{2,1,0:T(8,128)(2,1)S(1)} %and_select_fusion.gate_ref, bf16[8,104,2048]{2,1,0:T(8,128)(2,1)S(1)} %bitcast.58), custom_call_target="tpu_custom_call" | custom-call | flops 5000000000 | bytes 170000000 | tf_op jit(solution)/shard_map/give_back/pallas_call | solution.py:460
  339.5 0.7 copy.13
  340.2 3.2 multiply_bitcast_fusion
  343.3 0.8 copy.17
  (33 shorter events, 0.2 us)
Async XLA Ops:
  7.2 1.7 copy-start
  7.2 144.1 %all-gather.5.cloned.1.call-start = ((), (), s32[]{:S(2)}) async-start(), calls=%async_computation.4 | async-start | bytes 3604480 | tf_op jit(solution)/shard_map/all_gather | solution.py:495
  7.9 180.0 %reduce-scatter.5.cloned.1.call-start = ((), (), s32[]{:S(2)}) async-start(), calls=%async_computation.3 | async-start | bytes 3604480 | tf_op jit(solution)/shard_map/reduce_scatter | solution.py:541
  12.2 5.0 %copy-start.6 = (bf16[128,6]{0,1:T(8,128)(2,1)S(1)}, bf16[128,6]{0,1:T(8,128)(2,1)}, u32[]{:S(2)}) copy-start(bf16[128,6]{0,1:T(8,128)(2,1)} %param.10) | copy-start | bytes 4612
  12.2 5.3 %copy-start.1 = (bf16[128,2048]{1,0:T(8,128)(2,1)S(1)}, bf16[128,2048]{1,0:T(8,128)(2,1)}, u32[]{:S(2)}) copy-start(bf16[128,2048]{1,0:T(8,128)(2,1)} %dy_ref.1) | copy-start | bytes 1572868
  17.6 1.0 copy-start.2
  18.6 126.8 %copy-start.4 = (bf16[832,704]{0,1:T(8,128)(2,1)S(1)}, bf16[832,704]{0,1:T(8,128)(2,1)}, u32[]{:S(2)}) copy-start(bf16[832,704]{0,1:T(8,128)(2,1)} %copy.14) | copy-start | bytes 3514372
  18.6 126.8 %copy-start.5 = (bf16[832,704]{0,1:T(8,128)(2,1)S(1)}, bf16[832,704]{0,1:T(8,128)(2,1)}, u32[]{:S(2)}) copy-start(bf16[832,704]{0,1:T(8,128)(2,1)} %copy.15) | copy-start | bytes 3514372
  143.7 1.8 copy-start.3
  150.5 102.8 %all-gather.7.cloned.1.call-start = ((), (), s32[]{:S(2)}) async-start(), calls=%async_computation.5 | async-start | bytes 7208960 | tf_op jit(solution)/shard_map/all_gather | solution.py:496
  151.2 188.9 %reduce-scatter.3.cloned.1.call-start = ((), (), s32[]{:S(2)}) async-start(), calls=%async_computation.2 | async-start | bytes 7208960 | tf_op jit(solution)/shard_map/reduce_scatter | solution.py:535
  151.3 9.5 %copy-start.7 = (bf16[8,104,2048]{2,1,0:T(8,128)(2,1)S(1)}, bf16[8,104,2048]{2,1,0:T(8,128)(2,1)}, u32[]{:S(2)}) copy-start(bf16[8,104,2048]{2,1,0:T(8,128)(2,1)} %get-tuple-element.15) | copy-start | bytes 10223620
  159.4 1.0 copy-start.8
  159.4 1.4 copy-start.9
Sparse Core Ops, SparseCore 0:
  9.8 43.7 all-gather.4
  150.6 37.2 reduce-scatter.4
  189.7 63.5 all-gather.6
  255.7 62.9 reduce-scatter.2

commit v2 on v1

v2 whole, which is shorter than its diff:
```python
import functools

import jax
import jax.numpy as jnp
from jax import lax
from jax.experimental import pallas as pl
from jax.experimental.pallas import tpu as pltpu
from jax.sharding import PartitionSpec as P

MESH = pl.DeviceIdType.MESH
BF16, F32 = jnp.bfloat16, jnp.float32
NX, NZ, NC = 4, 8, 2
NY = 4
PEERS = NX * NC
LANES = 128
TOP = 6
GATE_LANE = 8
NT = (((1,), (1,)), ((), ()))
TN = (((0,), (0,)), ((), ()))


def place():
    e = lax.axis_index("expert")
    return e // (NZ * NC), lax.rem(e // NC, NZ), lax.rem(e, NC)


def device(x, z, c):
    return (lax.axis_index("dp"), (x * NZ + z) * NC + c)


def along_y(step):
    return (lax.rem(lax.axis_index("dp") + step, NY), lax.axis_index("expert"))


def enter(x, z, c):
    barrier = pltpu.get_barrier_semaphore()
    for step in (1, NZ - 1):
        pl.semaphore_signal(barrier, inc=1, device_id=device(x, lax.rem(z + step, NZ), c), device_id_type=MESH)
    for step in (1, NY - 1):
        pl.semaphore_signal(barrier, inc=1, device_id=along_y(step), device_id_type=MESH)
    me = x * NC + c
    for step in range(1, PEERS):
        peer = lax.rem(me + step, PEERS)
        pl.semaphore_signal(barrier, inc=1, device_id=device(peer // NC, z, lax.rem(peer, NC)), device_id_type=MESH)
    pl.semaphore_wait(barrier, 2 + 2 + PEERS - 1)


def aligned(index, size):
    return pl.ds(pl.multiple_of(index * size, size), size)


def front_kernel(
    chunks,
    cap,
    side_in,
    dy_in,
    x_in,
    saved,
    up_in,
    down_in,
    side_out,
    x_out,
    pre_out,
    gate_out,
    row_out,
    dn_out,
    *scratch,
):
    n = len(chunks)
    ring, stage = scratch[:n], scratch[n : 2 * n]
    (side_own, side_rows, dy_rows, pick, up, down, act, turned_act, coef_gate, coef_up) = scratch[2 * n : 2 * n + 10]
    z_send, z_recv, x_send, x_recv, own_sem, y_send, y_recv, y_own = scratch[2 * n + 10 :]
    ins, outs = (side_own, dy_in, x_in), (side_rows, dy_rows, x_out)
    x, z, c = place()
    y = lax.axis_index("dp")
    expert = lax.axis_index("expert")
    me = x * NC + c
    tok, width = dy_in.shape
    half_rows = tok // 2
    block = pick.shape[1]
    padded = dy_rows.shape[1]
    hidden = act.shape[1]
    sends = NZ - 1
    unit = NC * padded

    eye = (lax.broadcasted_iota(jnp.int32, (tok, tok), 0) == lax.broadcasted_iota(jnp.int32, (tok, tok), 1)).astype(BF16)
    side_own[...] = lax.dot_general(eye, side_in[...], NT, preferred_element_type=F32).astype(BF16)
    for segments, buf in ((s, b) for (s, _), b in zip(chunks, ring)):
        for array, col, w, off in segments:
            buf[z, :, off : off + w] = ins[array][:, col : col + w]
    for buf in outs:
        buf[:, block:, :] = jnp.zeros((PEERS, padded - block, buf.shape[2]), BF16)
    enter(x, z, c)

    weights = ((down_in, down), (up_in, up))

    def y_copy(k, hop):
        source, whole = weights[k]
        rows = whole.shape[1]
        cut = rows // 32 * 16
        first, second = (0, cut), (cut, rows - cut)
        lo, size = (first, second, second, first, first, second)[hop]
        step = 1 if hop in (0, 1, 4) else NY - 1
        back = NY - step
        slot = y if hop < 4 else lax.rem(y + back, NY)
        src = source.at[lo : lo + size, :] if hop < 4 else whole.at[slot, lo : lo + size, :]
        return pltpu.make_async_remote_copy(
            src_ref=src,
            dst_ref=whole.at[slot, lo : lo + size, :],
            send_sem=y_send.at[k, hop],
            recv_sem=y_recv.at[k, hop],
            device_id=along_y(step),
            device_id_type=MESH,
        )

    def y_own_copy(k):
        return pltpu.make_async_copy(weights[k][0], weights[k][1].at[y], y_own.at[k])

    def y_forward(k):
        y_copy(k, 0).wait_recv()
        y_copy(k, 4).start()
        y_copy(k, 2).wait_recv()
        y_copy(k, 5).start()

    def y_arrived(k):
        for hop in (1, 3, 4, 5):
            y_copy(k, hop).wait_recv()
        y_own_copy(k).wait()

    def hop(ch, way, i):
        step = 1 if way == 0 else NZ - 1
        dist = i // 2
        half = lax.rem(i + way, 2)
        blk = lax.rem(z + (NZ - step) * dist, NZ)
        view = ring[ch].at[blk, aligned(half, half_rows), :]
        return pltpu.make_async_remote_copy(
            src_ref=view,
            dst_ref=view,
            send_sem=z_send.at[ch, way, i],
            recv_sem=z_recv.at[ch, way, i],
            device_id=device(x, lax.rem(z + step, NZ), c),
            device_id_type=MESH,
        )

    def z_start(ch, i):
        for way in (0, 1):
            hop(ch, way, i).start()

    def z_arrived(ch, i):
        for way in (0, 1):
            hop(ch, way, i).wait_recv()

    def x_copies(ch, peer, slot, mark):
        made = []
        for array, col, w, off in chunks[ch][0]:
            kind = 0 if array == 0 else 1
            made.append(
                pltpu.make_async_remote_copy(
                    src_ref=stage[ch].at[peer, :, off : off + w],
                    dst_ref=outs[array].at[slot, 0:block, col : col + w],
                    send_sem=x_send.at[ch, kind, peer],
                    recv_sem=x_recv.at[ch, kind, mark],
                    device_id=device(peer // NC, z, lax.rem(peer, NC)),
                    device_id_type=MESH,
                )
            )
        return made

    def own_copies(ch):
        return [
            pltpu.make_async_copy(
                stage[ch].at[me, :, off : off + w],
                outs[array].at[me, 0:block, col : col + w],
                own_sem.at[ch, 0 if array == 0 else 1],
            )
            for array, col, w, off in chunks[ch][0]
        ]

    def make_pick():
        earlier = (
            lax.broadcasted_iota(jnp.int32, (tok, tok), 0) < lax.broadcasted_iota(jnp.int32, (tok, tok), 1)
        ).astype(BF16)
        slot_row = lax.broadcasted_iota(jnp.int32, (block, tok), 0).astype(F32)
        peer_row = lax.broadcasted_iota(jnp.int32, (PEERS, tok), 0)
        expert_row = ((peer_row // NC) * (NZ * NC) + z * NC + lax.rem(peer_row, NC)).astype(F32)
        turn = (
            lax.broadcasted_iota(jnp.int32, (LANES, LANES), 0) == lax.broadcasted_iota(jnp.int32, (LANES, LANES), 1)
        ).astype(BF16)

        def one(s, _):
            turned = lax.dot_general(turn, ring[0][s, :, 0:LANES], NT, preferred_element_type=F32)
            match = jnp.zeros((PEERS, tok), F32)
            for k in range(TOP):
                match = match + (jnp.broadcast_to(turned[k : k + 1, :], (PEERS, tok)) == expert_row).astype(F32)
            position = jnp.dot(match.astype(BF16), earlier, preferred_element_type=F32)
            slot = jnp.where(match > 0.0, position + (s * cap).astype(F32), -1.0)
            for peer in range(PEERS):
                hit = jnp.broadcast_to(slot[peer : peer + 1, :], (block, tok)) == slot_row
                pick[peer, :, aligned(s, tok)] = hit.astype(F32).astype(BF16)
            return 0

        lax.fori_loop(0, NZ, one, 0)
        side_out[...] = ring[0][:, :, 0:LANES]

    def pieces(ch, lo, hi):
        def one(peer, _):
            w_all = chunks[ch][1]
            rows = pick[peer]
            for at in range(0, w_all, 256):
                w = min(256, w_all - at)
                cols = ring[ch][:, :, at : at + w].reshape(NZ * tok, w)
                stage[ch][peer, :, at : at + w] = jnp.dot(rows, cols, preferred_element_type=F32).astype(BF16)

            @pl.when(peer != me)
            def _():
                for copy in x_copies(ch, peer, me, me):
                    copy.start()

            @pl.when(peer == me)
            def _():
                for copy in own_copies(ch):
                    copy.start()

            return 0

        lax.fori_loop(lo, hi, one, 0)

    def x_arrived(ch):
        def one(step, _):
            peer = lax.rem(me + step, PEERS)
            for copy in x_copies(ch, peer, peer, peer):
                copy.wait_recv()
            return 0

        lax.fori_loop(1, PEERS, one, 0)
        for copy in own_copies(ch):
            copy.wait()

    per_x = NZ * NC * cap
    new = lax.broadcasted_iota(jnp.int32, (unit, per_x), 0)
    old = lax.broadcasted_iota(jnp.int32, (unit, per_x), 1)
    core = (new >= padded).astype(jnp.int32)
    inner = new - core * padded

    def prepare(b):
        order = jnp.zeros((unit, per_x), jnp.bool_)
        for zed in range(NZ):
            order = order | (
                (inner >= zed * cap) & (inner < (zed + 1) * cap) & (old == inner + zed * (NC - 1) * cap + core * cap)
            )
        moved = jnp.dot(order.astype(F32).astype(BF16), saved[aligned(b, per_x), :], preferred_element_type=F32)
        gate, lift = moved[:, :hidden], moved[:, hidden:]
        sig = jax.nn.sigmoid(gate)
        rows = aligned(b, unit)
        swish = gate * sig
        act[rows, :] = (swish * lift).astype(BF16)
        coef_gate[rows, :] = lift * sig * (1.0 + gate * (1.0 - sig))
        coef_up[rows, :] = swish

    def through_down(b):
        rows = aligned(b, unit)
        two = pl.ds(b * NC, NC)
        dy = dy_rows[two, :, :].reshape(unit, width)
        act_grad = lax.dot_general(dy, down[...].reshape(hidden, width), NT, preferred_element_type=F32)
        gate_grad = jnp.sum(act[rows, :].astype(F32) * act_grad, axis=1, keepdims=True) / jnp.sqrt(F32(width))
        side = side_rows[two, :, :].reshape(unit, LANES).astype(F32)
        mine = expert.astype(F32)
        gain = jnp.zeros((unit, 1), F32)
        for k in range(TOP):
            gain = gain + jnp.where(side[:, k : k + 1] == mine, side[:, GATE_LANE + k : GATE_LANE + k + 1], 0.0)
        lane = lax.broadcasted_iota(jnp.int32, (unit, LANES), 1)
        gate_out[two, :, :] = (
            jnp.where((lane < TOP) & (side == mine), jnp.broadcast_to(gate_grad, (unit, LANES)), 0.0)
            .astype(BF16)
            .reshape(NC, padded, LANES)
        )
        scaled = gain * act_grad
        pre_out[rows, 0:hidden] = (scaled * coef_gate[rows, :]).astype(BF16)
        pre_out[rows, hidden : 2 * hidden] = (scaled * coef_up[rows, :]).astype(BF16)
        for at in range(0, width, 512):
            part = dy_rows[two, :, at : at + 512].reshape(unit, 512).astype(F32)
            dy_rows[two, :, at : at + 512] = (gain * part).astype(BF16).reshape(NC, padded, 512)

    def through_up(b):
        rows = aligned(b, unit)
        two = pl.ds(b * NC, NC)

        def one(q, _):
            grad = lax.dot_general(pre_out[rows, :], up[q], NT, preferred_element_type=F32)
            row_out[two, :, aligned(q, up.shape[1])] = grad.astype(BF16).reshape(NC, padded, up.shape[1])
            return 0

        lax.fori_loop(0, NY, one, 0)

    def down_grad(k):
        cols = aligned(k, 512)
        scaled_dy = dy_rows[:, :, cols].reshape(PEERS * padded, 512)
        dn_out[:, cols] = jnp.dot(turned_act[...], scaled_dy, preferred_element_type=F32).astype(BF16)

    def run(work, lo, hi):
        def one(b, _):
            work(b)
            return 0

        lax.fori_loop(lo, hi, one, 0)

    for k in (0, 1):
        y_own_copy(k).start()
        for h in (0, 2, 1, 3):
            y_copy(k, h).start()
    ticks = sends - 2
    for ch in range(n):
        z_start(ch, 0)
        z_start(ch, 1)
        if ch > 0:
            z_arrived(ch - 1, sends - 2)
            z_arrived(ch - 1, sends - 1)
        if ch == 1:
            make_pick()
        if ch in (1, 2):
            y_forward(ch - 1)

        def tick(i, _, ch=ch):
            z_arrived(ch, i)
            z_start(ch, i + 2)
            if ch == 0:
                run(prepare, (NX * i) // ticks, (NX * (i + 1)) // ticks)
            else:
                pieces(ch - 1, jnp.minimum(3 * i, PEERS), jnp.minimum(3 * i + 3, PEERS))
            return 0

        lax.fori_loop(0, ticks, tick, 0)
        if ch == 0:
            turned_act[...] = act[...].astype(F32).T.astype(BF16)
    z_arrived(n - 1, sends - 2)
    z_arrived(n - 1, sends - 1)
    pieces(n - 1, 0, PEERS)
    for ch in range(n // 2):
        x_arrived(ch)
    y_arrived(0)
    run(through_down, 0, NX)
    y_arrived(1)
    run(through_up, 0, NX)
    run(down_grad, 0, width // 512)
    for ch in range(n):
        if ch >= n // 2:
            x_arrived(ch)

        def drain(i, _, ch=ch):
            for way in (0, 1):
                hop(ch, way, i).wait_send()
            return 0

        lax.fori_loop(0, sends, drain, 0)

        def sent(step, _, ch=ch):
            peer = lax.rem(me + step, PEERS)
            for copy in x_copies(ch, peer, me, me):
                copy.wait_send()
            return 0

        lax.fori_loop(1, PEERS, sent, 0)
    for k in (0, 1):
        for h in range(6):
            y_copy(k, h).wait_send()


def front(side, dy, x, saved, up, down, cap):
    tok, width = dy.shape
    hidden = up.shape[1] // 2
    block = NZ * cap
    padded = -(-block // 16) * 16
    half = width // 2
    chunks = [
        ([(0, 0, LANES, 0), (1, 0, half, LANES)], LANES + half),
        ([(1, half, half, 0)], half),
        ([(2, 0, half, 0)], half),
        ([(2, half, half, 0)], half),
    ]
    n = len(chunks)
    rows = PEERS * padded
    vmem = pl.BlockSpec(memory_space=pltpu.VMEM)
    anywhere = pl.BlockSpec(memory_space=pl.ANY)
    shape = jax.ShapeDtypeStruct
    return pl.pallas_call(
        functools.partial(front_kernel, chunks, cap),
        out_shape=(
            shape((NZ, tok, LANES), BF16),
            shape((PEERS, padded, width), BF16),
            shape((rows, 2 * hidden), BF16),
            shape((PEERS, padded, LANES), BF16),
            shape((PEERS, padded, width), BF16),
            shape((hidden, width), BF16),
        ),
        in_specs=[vmem] * 4 + [anywhere] * 2,
        out_specs=(vmem,) * 6,
        scratch_shapes=[pltpu.VMEM((NZ, tok, w), BF16) for _, w in chunks]
        + [pltpu.VMEM((PEERS, block, w), BF16) for _, w in chunks]
        + [
            pltpu.VMEM((tok, LANES), BF16),
            pltpu.VMEM((PEERS, padded, LANES), BF16),
            pltpu.VMEM((PEERS, padded, width), BF16),
            pltpu.VMEM((PEERS, block, NZ * tok), BF16),
            pltpu.VMEM((NY,) + up.shape, BF16),
            pltpu.VMEM((NY,) + down.shape, BF16),
            pltpu.VMEM((rows, hidden), BF16),
            pltpu.VMEM((hidden, rows), BF16),
            pltpu.VMEM((rows, hidden), F32),
            pltpu.VMEM((rows, hidden), F32),
            pltpu.SemaphoreType.DMA((n, 2, NZ - 1)),
            pltpu.SemaphoreType.DMA((n, 2, NZ - 1)),
            pltpu.SemaphoreType.DMA((n, 2, PEERS)),
            pltpu.SemaphoreType.DMA((n, 2, PEERS)),
            pltpu.SemaphoreType.DMA((n, 2)),
            pltpu.SemaphoreType.DMA((2, 6)),
            pltpu.SemaphoreType.DMA((2, 6)),
            pltpu.SemaphoreType.DMA((2,)),
        ],
        compiler_params=pltpu.CompilerParams(collective_id=0, has_side_effects=True, vmem_limit_bytes=62 << 20),
        cost_estimate=pl.CostEstimate(flops=20_000_000_000, bytes_accessed=350_000_000, transcendentals=0),
        name="front",
    )(side, dy, x, saved, up, down)


def back_kernel(
    chunks, cap, scale, side_ref, gate_ref, row_ref, x_ref, pre_ref, gate_out, tok_out, gu_out, *scratch
):
    n = len(chunks)
    landed, total, leave, come = (scratch[k * n : (k + 1) * n] for k in range(4))
    spread, gu_leave, gu_come, z_send, z_recv, x_send, x_recv, own_sem, y_send, y_recv = scratch[4 * n :]
    ins, outs = (gate_ref, row_ref), (gate_out, tok_out)
    x, z, c = place()
    y = lax.axis_index("dp")
    me = x * NC + c
    tok = tok_out.shape[0]
    half_rows = tok // 2
    block = NZ * cap
    padded = row_ref.shape[1]
    pad = landed[0].shape[1]
    sends = NZ - 1

    for buf, (_, w) in zip(landed, chunks):
        buf[:, block:, :] = jnp.zeros((PEERS, pad - block, w), BF16)
    enter(x, z, c)

    def x_copies(ch, src_slot, dst_slot, mark, peer):
        made = []
        for array, col, w, off in chunks[ch][0]:
            made.append(
                pltpu.make_async_remote_copy(
                    src_ref=ins[array].at[src_slot, 0:block, col : col + w],
                    dst_ref=landed[ch].at[dst_slot, 0:block, off : off + w],
                    send_sem=x_send.at[ch, array, peer],
                    recv_sem=x_recv.at[ch, array, mark],
                    device_id=device(peer // NC, z, lax.rem(peer, NC)),
                    device_id_type=MESH,
                )
            )
        return made

    def own_copies(ch):
        return [
            pltpu.make_async_copy(
                ins[array].at[me, 0:block, col : col + w], landed[ch].at[me, 0:block, off : off + w], own_sem.at[ch, array]
            )
            for array, col, w, off in chunks[ch][0]
        ]

    for ch in range(n):

        def send(step, _, ch=ch):
            peer = lax.rem(me + step, PEERS)
            for copy in x_copies(ch, peer, me, me, peer):
                copy.start()
            return 0

        lax.fori_loop(1, PEERS, send, 0)
        for copy in own_copies(ch):
            copy.start()

    gu_rows = gu_out.shape[0]
    half_gu = gu_rows // 2

    def gu_part(ahead, half):
        first = lax.rem(y + ahead, NY) * gu_rows + half * half_gu
        cols = x_ref[:, :, pl.ds(pl.multiple_of(first, half_gu), half_gu)].reshape(PEERS * padded, half_gu)
        return lax.dot_general(cols, pre_ref[...], TN, preferred_element_type=F32)

    def gu_hop(k):
        return pltpu.make_async_remote_copy(
            src_ref=gu_leave.at[k],
            dst_ref=gu_come.at[k],
            send_sem=y_send.at[k],
            recv_sem=y_recv.at[k],
            device_id=along_y(1 if k < 3 else NY - 1),
            device_id_type=MESH,
        )

    def gu_send(k):
        up = k < 3
        ahead = 2 if k in (0, 3) else (1 if up else NY - 1)
        half = (0 if up else 1) if k in (0, 2, 3, 5) else (1 if up else 0)
        value = gu_part(ahead, half)
        if k in (2, 5):
            gu_hop(k - 2).wait_recv()
            value = value + gu_come[k - 2].astype(F32)
        gu_leave[k] = value.astype(BF16)
        gu_hop(k).start()

    def gu_own(half):
        gu_out[half * half_gu : (half + 1) * half_gu, :] = gu_part(0, half)

    def gu_finish():
        for half in (0, 1):
            rows = slice(half * half_gu, (half + 1) * half_gu)
            a, b = (2, 4) if half == 0 else (1, 5)
            gu_hop(a).wait_recv()
            gu_hop(b).wait_recv()
            gu_out[rows, :] = (gu_out[rows, :] + gu_come[a].astype(F32) + gu_come[b].astype(F32)) * scale

    gu_send(0)
    gu_send(3)

    later = (
        lax.broadcasted_iota(jnp.int32, (tok, tok), 1) < lax.broadcasted_iota(jnp.int32, (tok, tok), 0)
    ).astype(BF16)
    lane = lax.broadcasted_iota(jnp.int32, (tok, LANES), 1)
    expert_lane = jnp.where(lane < PEERS, (lane // NC) * (NZ * NC) + z * NC + lax.rem(lane, NC), -1).astype(F32)
    slot_lane = lax.broadcasted_iota(jnp.int32, (tok, pad), 1).astype(F32)

    def spread_one(s, _):
        side = side_ref[s].astype(F32)
        match = jnp.zeros((tok, LANES), F32)
        for k in range(TOP):
            match = match + (jnp.broadcast_to(side[:, k : k + 1], (tok, LANES)) == expert_lane).astype(F32)
        position = jnp.dot(later, match.astype(BF16), preferred_element_type=F32)
        slot = jnp.where(match > 0.0, position + (s * cap).astype(F32), -1.0)
        for peer in range(PEERS):
            hit = jnp.broadcast_to(slot[:, peer : peer + 1], (tok, pad)) == slot_lane
            spread[s, :, peer * pad : (peer + 1) * pad] = hit.astype(F32).astype(BF16)
        return 0

    lax.fori_loop(0, NZ, spread_one, 0)

    def x_arrived(ch):
        def one(step, _):
            peer = lax.rem(me + step, PEERS)
            for copy in x_copies(ch, peer, peer, peer, peer):
                copy.wait_recv()
            return 0

        lax.fori_loop(1, PEERS, one, 0)
        for copy in own_copies(ch):
            copy.wait()

    def combines(ch, lo, hi):
        def one(k, _):
            width = chunks[ch][1]
            s = lax.rem(z + NZ // 2 + k, NZ)
            rows = spread[s]
            for at in range(0, width, 256):
                w = min(256, width - at)
                cols = landed[ch][:, :, at : at + w].reshape(PEERS * pad, w)
                total[ch][s, :, at : at + w] = jnp.dot(rows, cols, preferred_element_type=F32)
            return 0

        lax.fori_loop(lo, hi, one, 0)

    def hop(ch, way, i):
        step = 1 if way == 0 else NZ - 1
        return pltpu.make_async_remote_copy(
            src_ref=leave[ch].at[way, i],
            dst_ref=come[ch].at[way, i],
            send_sem=z_send.at[ch, way, i],
            recv_sem=z_recv.at[ch, way, i],
            device_id=device(x, lax.rem(z + step, NZ), c),
            device_id_type=MESH,
        )

    def z_step(ch, i, first):
        for way in (0, 1):
            step = 1 if way == 0 else NZ - 1
            dist = NZ // 2 - (i + 1) // 2
            half = lax.rem(i + way, 2)
            s = lax.rem(z + step * dist, NZ)
            value = total[ch][s, aligned(half, half_rows), :]
            if not first:
                hop(ch, way, i - 2).wait_recv()
                value = value + come[ch][way, i - 2].astype(F32)
            leave[ch][way, i] = value.astype(BF16)
            hop(ch, way, i).start()

    def finish(ch):
        for way in (0, 1):
            hop(ch, way, sends - 2).wait_recv()
            hop(ch, way, sends - 1).wait_recv()
        for half in (0, 1):
            rows = slice(half * half_rows, (half + 1) * half_rows)
            value = total[ch][z, rows, :]
            for way in (0, 1):
                i = sends - 1 if (sends - 1 + way) % 2 == half else sends - 2
                value = value + come[ch][way, i].astype(F32)
            for array, col, w, off in chunks[ch][0]:
                outs[array][rows, col : col + w] = value[:, off : off + w].astype(BF16)

    x_arrived(0)
    combines(0, 0, NZ)
    ticks = sends - 2
    extra = {0: (lambda: gu_send(1), lambda: gu_send(4)), 1: (lambda: gu_send(2), lambda: gu_send(5)), 2: (lambda: gu_own(0), lambda: gu_own(1))}
    for ch in range(n):
        z_step(ch, 0, True)
        z_step(ch, 1, True)
        if ch > 0:
            finish(ch - 1)
        for work in extra.get(ch, ()):
            work()
        if ch + 1 < n:
            x_arrived(ch + 1)

        def tick(i, _, ch=ch):
            z_step(ch, i + 2, False)
            if ch + 1 < n:
                combines(ch + 1, (NZ * i) // ticks, (NZ * (i + 1)) // ticks)
            return 0

        lax.fori_loop(0, ticks, tick, 0)
    finish(n - 1)
    gu_finish()
    for ch in range(n):

        def drain(i, _, ch=ch):
            for way in (0, 1):
                hop(ch, way, i).wait_send()
            return 0

        lax.fori_loop(0, sends, drain, 0)

        def sent(step, _, ch=ch):
            peer = lax.rem(me + step, PEERS)
            for copy in x_copies(ch, peer, me, me, peer):
                copy.wait_send()
            return 0

        lax.fori_loop(1, PEERS, sent, 0)
    for k in range(6):
        gu_hop(k).wait_send()


def back(side, gate_rows, rows, x_rows, pre, cap, gu_rows, scale):
    width = rows.shape[2]
    tok = side.shape[1]
    pad = -(-NZ * cap // LANES) * LANES
    quarter = width // 4
    chunks = [([(0, 0, LANES, 0), (1, 0, quarter, LANES)], LANES + quarter)]
    chunks += [([(1, k * quarter, quarter, 0)], quarter) for k in (1, 2, 3)]
    n = len(chunks)
    vmem = pl.BlockSpec(memory_space=pltpu.VMEM)
    shape = jax.ShapeDtypeStruct
    return pl.pallas_call(
        functools.partial(back_kernel, chunks, cap, scale),
        out_shape=(shape((tok, LANES), BF16), shape((tok, width), BF16), shape((gu_rows, pre.shape[1]), F32)),
        in_specs=[vmem] * 5,
        out_specs=(vmem,) * 3,
        scratch_shapes=[pltpu.VMEM((PEERS, pad, w), BF16) for _, w in chunks]
        + [pltpu.VMEM((NZ, tok, w), F32) for _, w in chunks]
        + [pltpu.VMEM((2, NZ - 1, tok // 2, w), BF16) for _, w in chunks] * 2
        + [
            pltpu.VMEM((NZ, tok, PEERS * pad), BF16),
            pltpu.VMEM((6, gu_rows // 2, pre.shape[1]), BF16),
            pltpu.VMEM((6, gu_rows // 2, pre.shape[1]), BF16),
            pltpu.SemaphoreType.DMA((n, 2, NZ - 1)),
            pltpu.SemaphoreType.DMA((n, 2, NZ - 1)),
            pltpu.SemaphoreType.DMA((n, 2, PEERS)),
            pltpu.SemaphoreType.DMA((n, 2, PEERS)),
            pltpu.SemaphoreType.DMA((n, 2)),
            pltpu.SemaphoreType.DMA((6,)),
            pltpu.SemaphoreType.DMA((6,)),
        ],
        compiler_params=pltpu.CompilerParams(collective_id=1, has_side_effects=True, vmem_limit_bytes=62 << 20),
        cost_estimate=pl.CostEstimate(flops=10_000_000_000, bytes_accessed=250_000_000, transcendentals=0),
        name="back",
    )(side, gate_rows, rows, x_rows, pre)


def on_device(tokens, out_grad, routes, gate_weights, saved_preacts, gate_up, down_proj):
    groups = lax.axis_size("dp")
    tok_rows, top = routes.shape
    cap = saved_preacts.shape[2] // lax.axis_size("expert")
    zeros = functools.partial(jnp.zeros, dtype=BF16)
    side = jnp.concatenate(
        [
            routes.T.astype(BF16),
            zeros((GATE_LANE - top, tok_rows)),
            gate_weights.T,
            zeros((LANES - GATE_LANE - top, tok_rows)),
        ]
    )
    sides, x_rows, pre, gate_rows, rows, grad_dn = front(
        side, out_grad, tokens, saved_preacts[0, 0], gate_up[0], down_proj[0], cap
    )
    grad_scale = float(1.0 / (groups * tok_rows * top) ** 0.5)
    grad_dn = lax.psum_scatter(grad_dn, "dp", scatter_dimension=0, tiled=True).astype(F32) * grad_scale
    gates, grad_tokens, grad_gu = back(sides, gate_rows, rows, x_rows, pre, cap, gate_up.shape[1], grad_scale)
    return (grad_tokens, gates[:, :top], grad_gu[None], grad_dn[None])


def solution(mesh):
    in_specs = (
        P(("dp", "expert"), None),
        P(("dp", "expert"), None),
        P(("dp", "expert"), None),
        P(("dp", "expert"), None),
        P("dp", "expert", None, None),
        P("expert", "dp", None),
        P("expert", "dp", None),
    )
    out_specs = (
        P(("dp", "expert"), None),
        P(("dp", "expert"), None),
        P("expert", "dp", None),
        P("expert", "dp", None),
    )
    return jax.shard_map(
        on_device, mesh=mesh, in_specs=in_specs, out_specs=out_specs, check_vma=False
    )
```

time: 351 us -> 238 us (0.68)
  waiting for transfers between devices: 82.6 us -> 0.02 us
  matrix products: 31.7 us -> 0 us
  Pallas kernels: 203 us -> 214 us
  local copies, waits for them, and re-layouts: 12.6 us -> 5.19 us
    all_gather x2 -> x0, waiting for transfers between devices: 63 us -> none  [the longest x1 63 us: on_device(): up = lax.all_gather(gate_up[0], 'dp', axis=0, tiled=True)]
    dot_general x5 -> x0, matrix products: 31.7 us -> none  [the longest x1 8.69 us: on_device(): lax.dot_general(pre_grad, up, (((1,), (1,)), ((), ())), preferred_element...]
    reduce_scatter x2 -> x1, waiting for transfers between devices: 18.2 us -> 0.01 us  [on_device(): lax.psum_scatter(grad_dn, 'dp', scatter_dimension=0, tiled=True).astype(F32)]
    pallas_call x2, Pallas kernels: 203 us -> 214 us  [the longest x1 125 us: front(): pl.pallas_call(functools.partial(front_kernel, chunks, cap), out_shape=(s...]
    unnamed x24 -> x5, local copies, waits for them, and re-layouts: 10.5 us -> 5.03 us
  transfers between devices with their start and end apart: 4 -> 1, of which waited for: 2 -> 0; matrix products, arithmetic and copies ran while one was open for 12% -> 1% of each run, Pallas kernels for 58% -> 37%
where the time goes in v2:
time: 238 us
  Pallas kernels  214 us (90%)
  between operations  14.1 us (6%)
  local copies, waits for them, and re-layouts  5.19 us (2%)
  other arithmetic  4.47 us (2%)
    pallas_call x1, Pallas kernels, front(): pl.pallas_call(functools.partial(front_kernel, chunks, cap), out_shape=(s...  125 us
    pallas_call x1, Pallas kernels, back(): pl.pallas_call(functools.partial(back_kernel, chunks, cap, scale), out_sh...  88.9 us
    unnamed x5, local copies, waits for them, and re-layouts  5.03 us
  transfers between devices with their start and end apart: 1, of which 0 were waited for; matrix products, arithmetic and copies ran while one was open for 1% of the time, Pallas kernels for 37%

profile of v2, /device:TPU:1, one launch (start us, length us, event | category | flops | bytes accessed | tf_op | source)
XLA Modules:
  0.0 237.8 jit_solution(3532912046575515869)
XLA Ops:
  7.2 0.0 reduce-scatter.2.cloned.1.call-start
  7.2 0.1 pad.3.clone
  7.3 0.1 pad.1.clone
  7.4 0.7 convert_bitcast_fusion
  8.1 1.4 maximum_maximum_fusion.side_in
  9.5 125.1 %front.1 = (bf16[8,128,128]{2,1,0:T(8,128)(2,1)}, bf16[8,112,2048]{2,1,0:T(8,128)(2,1)}, bf16[896,1408]{1,0:T(8,128)(2,1)}, bf16[8,112,128]{2,1,0:T(8,128)(2,1)}...) custom-call(bf16[128,128]{1,0:T(8,128)(2,1)} %maximum_maximum_fusion.side_in, bf16[128,2048]{1,0:T(8,128)(2,1)} %dy_in.1, ...), custom_call_target="tpu_custom_call" | custom-call | flops 20000000000 | bytes 350000000 | tf_op jit(solution)/shard_map/front/pallas_call | solution.py:385
  134.6 0.0 reduce-scatter.2.cloned.1.call-update
  134.6 88.9 %back.1 = (bf16[128,128]{1,0:T(8,128)(2,1)}, bf16[128,2048]{1,0:T(8,128)(2,1)}, f32[512,1408]{1,0:T(8,128)}) custom-call(bf16[8,128,128]{2,1,0:T(8,128)(2,1)} %get-tuple-element.13.side_ref, bf16[8,112,128]{2,1,0:T(8,128)(2,1)} %get-tuple-element.14.gate_ref, bf16[8,112,2048]{2,1,0:T(8,128)(2,1)} %get-tuple-element.15.row_ref, ...), custom_call_target="tpu_custom_call" | custom-call | flops 10000000000 | bytes 250000000 | tf_op jit(solution)/shard_map/back/pallas_call | solution.py:659
  223.5 0.0 copy-start
  223.6 1.6 copy.11
  225.1 0.0 reduce-scatter.2.cloned.1.call-done
  225.1 2.4 %multiply_bitcast_fusion = f32[1,176,2048]{2,1,0:T(8,128)} fusion(bf16[176,2048]{1,0:T(8,128)(2,1)} %reduce-scatter.2.cloned.1.call-done), kind=kLoop, calls=%fused_computation | loop fusion | flops 720896 | bytes 2162688 | tf_op jit(solution)/shard_map/broadcast_in_dim | solution.py:704
  227.5 1.9 copy.14
  229.4 0.0 copy-done
  229.4 1.6 copy.15
  (2 shorter events, 0.0 us)
Async XLA Ops:
  7.2 218.0 %reduce-scatter.2.cloned.1.call-start = ((), (), s32[]{:S(2)}) async-start(), calls=%async_computation.1 | async-start | bytes 3604480 | tf_op jit(solution)/shard_map/reduce_scatter | solution.py:702
  223.5 5.8 %copy-start = (f32[512,1408]{1,0:T(8,128)S(1)}, f32[512,1408]{1,0:T(8,128)}, u32[]{:S(2)}) copy-start(f32[512,1408]{1,0:T(8,128)} %get-tuple-element.20) | copy-start | bytes 8650756
Sparse Core Ops, SparseCore 0:
  134.7 62.0 reduce-scatter.1

commit v3 on v2

--- a/solution.py
+++ b/solution.py
@@ -14,6 +14,8 @@
 PEERS = NX * NC
 LANES = 128
 TOP = 6
+DY_CHUNKS, X_CHUNKS = (512, 768, 768), (768, 768, 512)
+BACK_CHUNKS = (256, 384, 512, 512, 384)
 GATE_LANE = 8
 NT = (((1,), (1,)), ((), ()))
 TN = (((0,), (0,)), ((), ()))
@@ -52,6 +54,7 @@
 def front_kernel(
     chunks,
     cap,
+    scale,
     side_in,
     dy_in,
     x_in,
@@ -67,9 +70,10 @@
     *scratch,
 ):
     n = len(chunks)
-    ring, stage = scratch[:n], scratch[n : 2 * n]
-    (side_own, side_rows, dy_rows, pick, up, down, act, turned_act, coef_gate, coef_up) = scratch[2 * n : 2 * n + 10]
-    z_send, z_recv, x_send, x_recv, own_sem, y_send, y_recv, y_own = scratch[2 * n + 10 :]
+    ring, stage = scratch[:n], scratch[n : n + n // 2] * 2
+    later = scratch[n + n // 2 :]
+    side_own, side_rows, dy_rows, scaled_rows, pick, up, down, act, turned_act, coef_gate, coef_up, dn, dn_come, dn_sum = later[:14]
+    z_send, z_recv, x_send, x_recv, own_sem, y_send, y_recv, y_own, d_send, d_recv = later[14:]
     ins, outs = (side_own, dy_in, x_in), (side_rows, dy_rows, x_out)
     x, z, c = place()
     y = lax.axis_index("dp")
@@ -225,17 +229,6 @@
 
         lax.fori_loop(lo, hi, one, 0)
 
-    def x_arrived(ch):
-        def one(step, _):
-            peer = lax.rem(me + step, PEERS)
-            for copy in x_copies(ch, peer, peer, peer):
-                copy.wait_recv()
-            return 0
-
-        lax.fori_loop(1, PEERS, one, 0)
-        for copy in own_copies(ch):
-            copy.wait()
-
     per_x = NZ * NC * cap
     new = lax.broadcasted_iota(jnp.int32, (unit, per_x), 0)
     old = lax.broadcasted_iota(jnp.int32, (unit, per_x), 1)
@@ -257,17 +250,28 @@
         coef_gate[rows, :] = lift * sig * (1.0 + gate * (1.0 - sig))
         coef_up[rows, :] = swish
 
+    def gain_of(b):
+        side = side_rows[pl.ds(b * NC, NC), :, :].reshape(unit, LANES).astype(F32)
+        mine = expert.astype(F32)
+        gain = jnp.zeros((unit, 1), F32)
+        for k in range(TOP):
+            gain = gain + jnp.where(side[:, k : k + 1] == mine, side[:, GATE_LANE + k : GATE_LANE + k + 1], 0.0)
+        return side, mine, gain
+
+    def scale_rows(b):
+        two = pl.ds(b * NC, NC)
+        gain = gain_of(b)[2]
+        for at in range(0, width, 512):
+            part = dy_rows[two, :, at : at + 512].reshape(unit, 512).astype(F32)
+            scaled_rows[two, :, at : at + 512] = (gain * part).astype(BF16).reshape(NC, padded, 512)
+
     def through_down(b):
         rows = aligned(b, unit)
         two = pl.ds(b * NC, NC)
         dy = dy_rows[two, :, :].reshape(unit, width)
         act_grad = lax.dot_general(dy, down[...].reshape(hidden, width), NT, preferred_element_type=F32)
         gate_grad = jnp.sum(act[rows, :].astype(F32) * act_grad, axis=1, keepdims=True) / jnp.sqrt(F32(width))
-        side = side_rows[two, :, :].reshape(unit, LANES).astype(F32)
-        mine = expert.astype(F32)
-        gain = jnp.zeros((unit, 1), F32)
-        for k in range(TOP):
-            gain = gain + jnp.where(side[:, k : k + 1] == mine, side[:, GATE_LANE + k : GATE_LANE + k + 1], 0.0)
+        side, mine, gain = gain_of(b)
         lane = lax.broadcasted_iota(jnp.int32, (unit, LANES), 1)
         gate_out[two, :, :] = (
             jnp.where((lane < TOP) & (side == mine), jnp.broadcast_to(gate_grad, (unit, LANES)), 0.0)
@@ -277,9 +281,6 @@
         scaled = gain * act_grad
         pre_out[rows, 0:hidden] = (scaled * coef_gate[rows, :]).astype(BF16)
         pre_out[rows, hidden : 2 * hidden] = (scaled * coef_up[rows, :]).astype(BF16)
-        for at in range(0, width, 512):
-            part = dy_rows[two, :, at : at + 512].reshape(unit, 512).astype(F32)
-            dy_rows[two, :, at : at + 512] = (gain * part).astype(BF16).reshape(NC, padded, 512)
 
     def through_up(b):
         rows = aligned(b, unit)
@@ -294,8 +295,45 @@
 
     def down_grad(k):
         cols = aligned(k, 512)
-        scaled_dy = dy_rows[:, :, cols].reshape(PEERS * padded, 512)
-        dn_out[:, cols] = jnp.dot(turned_act[...], scaled_dy, preferred_element_type=F32).astype(BF16)
+        scaled_dy = scaled_rows[:, :, cols].reshape(PEERS * padded, 512)
+        dn[:, :, cols] = (
+            jnp.dot(turned_act[...], scaled_dy, preferred_element_type=F32).astype(BF16).reshape(NY, hidden // NY, 512)
+        )
+
+    dn_rows = hidden // NY
+    dn_cut = dn_rows // 32 * 16
+    spans = ((0, dn_cut), (dn_cut, dn_rows - dn_cut))
+
+    def dn_hop(k):
+        lo, size = spans[(0, 1, 0, 1, 0, 1)[k]]
+        src = dn_sum.at[k // 3, 0:size, :]
+        if k in (0, 1, 3, 4):
+            ahead = (2, 1, 0, 2, NY - 1)[k]
+            src = dn.at[lax.rem(y + ahead, NY), lo : lo + size, :]
+        return pltpu.make_async_remote_copy(
+            src_ref=src,
+            dst_ref=dn_come.at[k, 0:size, :],
+            send_sem=d_send.at[k],
+            recv_sem=d_recv.at[k],
+            device_id=along_y(1 if k < 3 else NY - 1),
+            device_id_type=MESH,
+        )
+
+    def dn_pass_on():
+        for k in (2, 5):
+            lo, size = spans[0 if k == 2 else 1]
+            dn_hop(k - 2).wait_recv()
+            own = dn[lax.rem(y + (1 if k == 2 else NY - 1), NY), lo : lo + size, :].astype(F32)
+            dn_sum[k // 3, 0:size, :] = (own + dn_come[k - 2, 0:size, :].astype(F32)).astype(BF16)
+            dn_hop(k).start()
+
+    def dn_finish():
+        for (lo, size), (a, b) in zip(spans, ((2, 4), (1, 5))):
+            dn_hop(a).wait_recv()
+            dn_hop(b).wait_recv()
+            value = dn[y, lo : lo + size, :].astype(F32)
+            value = value + dn_come[a, 0:size, :].astype(F32) + dn_come[b, 0:size, :].astype(F32)
+            dn_out[lo : lo + size, :] = value * scale
 
     def run(work, lo, hi):
         def one(b, _):
@@ -309,42 +347,100 @@
         for h in (0, 2, 1, 3):
             y_copy(k, h).start()
     ticks = sends - 2
+    half_n = n // 2
+
+    def drained(ch):
+        def sent(step, _):
+            peer = lax.rem(me + step, PEERS)
+            for copy in x_copies(ch, peer, me, me):
+                copy.wait_send()
+            return 0
+
+        lax.fori_loop(1, PEERS, sent, 0)
+
+    def own_landed(ch):
+        for copy in own_copies(ch):
+            copy.wait()
+
+    def free_stage(ch):
+        if ch >= half_n:
+            drained(ch - half_n)
+
+    def x_landed(ch):
+        def one(step, _):
+            peer = lax.rem(me + step, PEERS)
+            for copy in x_copies(ch, peer, peer, peer):
+                copy.wait_recv()
+            return 0
+
+        lax.fori_loop(1, PEERS, one, 0)
+
+    z_start(0, 0)
+    z_start(0, 1)
     for ch in range(n):
-        z_start(ch, 0)
-        z_start(ch, 1)
         if ch > 0:
             z_arrived(ch - 1, sends - 2)
             z_arrived(ch - 1, sends - 1)
+            free_stage(ch - 1)
+        if ch > 1:
+            own_landed(ch - 2)
         if ch == 1:
             make_pick()
-        if ch in (1, 2):
-            y_forward(ch - 1)
+        if ch in (2, 3):
+            y_forward(ch - 2)
 
         def tick(i, _, ch=ch):
             z_arrived(ch, i)
             z_start(ch, i + 2)
+            if ch + 1 < n:
+
+                @pl.when(i >= ticks - 2)
+                def _():
+                    z_start(ch + 1, i - (ticks - 2))
+
             if ch == 0:
                 run(prepare, (NX * i) // ticks, (NX * (i + 1)) // ticks)
             else:
-                pieces(ch - 1, jnp.minimum(3 * i, PEERS), jnp.minimum(3 * i + 3, PEERS))
+                pieces(ch - 1, jnp.minimum(4 * i, PEERS), jnp.minimum(4 * i + 4, PEERS))
+            if ch == half_n + 1:
+
+                @pl.when(i == 2)
+                def _():
+                    for k in range(half_n):
+                        x_landed(k)
+                    run(scale_rows, 0, NX)
+
+                tiles = width // 512
+                run(down_grad, jnp.clip(2 * (i - 3), 0, tiles), jnp.clip(2 * (i - 2), 0, tiles))
+            if ch == n - 1:
+
+                @pl.when(i == 0)
+                def _():
+                    y_arrived(0)
+
+                run(through_down, jnp.maximum(i - 1, 0), i)
             return 0
 
         lax.fori_loop(0, ticks, tick, 0)
         if ch == 0:
             turned_act[...] = act[...].astype(F32).T.astype(BF16)
+        if ch == half_n + 1:
+            for k in (0, 3, 1, 4):
+                dn_hop(k).start()
     z_arrived(n - 1, sends - 2)
     z_arrived(n - 1, sends - 1)
+    free_stage(n - 1)
     pieces(n - 1, 0, PEERS)
-    for ch in range(n // 2):
-        x_arrived(ch)
-    y_arrived(0)
-    run(through_down, 0, NX)
+    dn_pass_on()
     y_arrived(1)
     run(through_up, 0, NX)
-    run(down_grad, 0, width // 512)
+    dn_finish()
     for ch in range(n):
-        if ch >= n // 2:
-            x_arrived(ch)
+        if ch >= half_n:
+            x_landed(ch)
+            drained(ch)
+        if ch >= n - 2:
+            own_landed(ch)
 
         def drain(i, _, ch=ch):
             for way in (0, 1):
@@ -352,53 +448,49 @@
             return 0
 
         lax.fori_loop(0, sends, drain, 0)
-
-        def sent(step, _, ch=ch):
-            peer = lax.rem(me + step, PEERS)
-            for copy in x_copies(ch, peer, me, me):
-                copy.wait_send()
-            return 0
-
-        lax.fori_loop(1, PEERS, sent, 0)
     for k in (0, 1):
         for h in range(6):
             y_copy(k, h).wait_send()
-
-
-def front(side, dy, x, saved, up, down, cap):
+    for k in range(6):
+        dn_hop(k).wait_send()
+
+
+def front(side, dy, x, saved, up, down, cap, scale):
     tok, width = dy.shape
     hidden = up.shape[1] // 2
     block = NZ * cap
     padded = -(-block // 16) * 16
-    half = width // 2
-    chunks = [
-        ([(0, 0, LANES, 0), (1, 0, half, LANES)], LANES + half),
-        ([(1, half, half, 0)], half),
-        ([(2, 0, half, 0)], half),
-        ([(2, half, half, 0)], half),
-    ]
+    chunks = []
+    for array, widths in ((1, DY_CHUNKS), (2, X_CHUNKS)):
+        col = 0
+        for w in widths:
+            off = 0 if chunks else LANES
+            chunks.append(([(0, 0, LANES, 0)] * (off > 0) + [(array, col, w, off)], off + w))
+            col += w
     n = len(chunks)
     rows = PEERS * padded
+    dn_part = hidden // NY - hidden // NY // 32 * 16
     vmem = pl.BlockSpec(memory_space=pltpu.VMEM)
     anywhere = pl.BlockSpec(memory_space=pl.ANY)
     shape = jax.ShapeDtypeStruct
     return pl.pallas_call(
-        functools.partial(front_kernel, chunks, cap),
+        functools.partial(front_kernel, chunks, cap, scale),
         out_shape=(
             shape((NZ, tok, LANES), BF16),
             shape((PEERS, padded, width), BF16),
             shape((rows, 2 * hidden), BF16),
             shape((PEERS, padded, LANES), BF16),
             shape((PEERS, padded, width), BF16),
-            shape((hidden, width), BF16),
+            shape((hidden // NY, width), F32),
         ),
         in_specs=[vmem] * 4 + [anywhere] * 2,
         out_specs=(vmem,) * 6,
         scratch_shapes=[pltpu.VMEM((NZ, tok, w), BF16) for _, w in chunks]
-        + [pltpu.VMEM((PEERS, block, w), BF16) for _, w in chunks]
+        + [pltpu.VMEM((PEERS, block, max(a[1], b[1])), BF16) for a, b in zip(chunks[: n // 2], chunks[n // 2 :])]
         + [
             pltpu.VMEM((tok, LANES), BF16),
             pltpu.VMEM((PEERS, padded, LANES), BF16),
+            pltpu.VMEM((PEERS, padded, width), BF16),
             pltpu.VMEM((PEERS, padded, width), BF16),
             pltpu.VMEM((PEERS, block, NZ * tok), BF16),
             pltpu.VMEM((NY,) + up.shape, BF16),
@@ -407,6 +499,9 @@
             pltpu.VMEM((hidden, rows), BF16),
             pltpu.VMEM((rows, hidden), F32),
             pltpu.VMEM((rows, hidden), F32),
+            pltpu.VMEM((NY, hidden // NY, width), BF16),
+            pltpu.VMEM((6, dn_part, width), BF16),
+            pltpu.VMEM((2, dn_part, width), BF16),
             pltpu.SemaphoreType.DMA((n, 2, NZ - 1)),
             pltpu.SemaphoreType.DMA((n, 2, NZ - 1)),
             pltpu.SemaphoreType.DMA((n, 2, PEERS)),
@@ -415,6 +510,8 @@
             pltpu.SemaphoreType.DMA((2, 6)),
             pltpu.SemaphoreType.DMA((2, 6)),
             pltpu.SemaphoreType.DMA((2,)),
+            pltpu.SemaphoreType.DMA((6,)),
+            pltpu.SemaphoreType.DMA((6,)),
         ],
         compiler_params=pltpu.CompilerParams(collective_id=0, has_side_effects=True, vmem_limit_bytes=62 << 20),
         cost_estimate=pl.CostEstimate(flops=20_000_000_000, bytes_accessed=350_000_000, transcendentals=0),
@@ -466,9 +563,8 @@
             for array, col, w, off in chunks[ch][0]
         ]
 
-    for ch in range(n):
-
-        def send(step, _, ch=ch):
+    def x_start(ch):
+        def send(step, _):
             peer = lax.rem(me + step, PEERS)
             for copy in x_copies(ch, peer, me, me, peer):
                 copy.start()
@@ -477,6 +573,9 @@
         lax.fori_loop(1, PEERS, send, 0)
         for copy in own_copies(ch):
             copy.start()
+
+    x_start(0)
+    x_start(1)
 
     gu_rows = gu_out.shape[0]
     half_gu = gu_rows // 2
@@ -567,7 +666,7 @@
         lax.fori_loop(lo, hi, one, 0)
 
     def hop(ch, way, i):
-        step = 1 if way == 0 else NZ - 1
+        step = 1 + way * (NZ - 2)
         return pltpu.make_async_remote_copy(
             src_ref=leave[ch].at[way, i],
             dst_ref=come[ch].at[way, i],
@@ -577,18 +676,21 @@
             device_id_type=MESH,
         )
 
-    def z_step(ch, i, first):
-        for way in (0, 1):
-            step = 1 if way == 0 else NZ - 1
-            dist = NZ // 2 - (i + 1) // 2
+    def z_step(ch, i):
+        dist = NZ // 2 - (i + 1) // 2
+
+        def one(way, _):
+            s = lax.rem(z + (1 + way * (NZ - 2)) * dist, NZ)
             half = lax.rem(i + way, 2)
-            s = lax.rem(z + step * dist, NZ)
             value = total[ch][s, aligned(half, half_rows), :]
-            if not first:
+            if i >= 2:
                 hop(ch, way, i - 2).wait_recv()
                 value = value + come[ch][way, i - 2].astype(F32)
             leave[ch][way, i] = value.astype(BF16)
             hop(ch, way, i).start()
+            return 0
+
+        lax.fori_loop(0, 2, one, 0)
 
     def finish(ch):
         for way in (0, 1):
@@ -603,27 +705,33 @@
             for array, col, w, off in chunks[ch][0]:
                 outs[array][rows, col : col + w] = value[:, off : off + w].astype(BF16)
 
+    x_start(2)
     x_arrived(0)
     combines(0, 0, NZ)
-    ticks = sends - 2
-    extra = {0: (lambda: gu_send(1), lambda: gu_send(4)), 1: (lambda: gu_send(2), lambda: gu_send(5)), 2: (lambda: gu_own(0), lambda: gu_own(1))}
-    for ch in range(n):
-        z_step(ch, 0, True)
-        z_step(ch, 1, True)
-        if ch > 0:
-            finish(ch - 1)
-        for work in extra.get(ch, ()):
-            work()
-        if ch + 1 < n:
-            x_arrived(ch + 1)
-
-        def tick(i, _, ch=ch):
-            z_step(ch, i + 2, False)
+    period = NZ // 2
+    extra = {
+        0: ((gu_send, 1), (gu_send, 4)),
+        1: ((gu_send, 2), (gu_send, 5)),
+        2: ((gu_own, 0), (gu_own, 1)),
+    }
+    for tick in range(period * (n - 1) + sends):
+        ch, r = divmod(tick, period)
+        for k, i in ((ch - 1, r + period), (ch, r)):
+            if 0 <= k < n and i < sends:
+                z_step(k, i)
+        if ch < n:
+            if r == 0 and ch + 1 < n:
+                x_arrived(ch + 1)
+                if ch + 3 < n:
+                    x_start(ch + 3)
             if ch + 1 < n:
-                combines(ch + 1, (NZ * i) // ticks, (NZ * (i + 1)) // ticks)
-            return 0
-
-        lax.fori_loop(0, ticks, tick, 0)
+                combines(ch + 1, NZ * r // period, NZ * (r + 1) // period)
+            if r == 1 and ch > 1:
+                finish(ch - 2)
+            if r in (1, 3) and ch in extra:
+                work, arg = extra[ch][r // 2]
+                work(arg)
+    finish(n - 2)
     finish(n - 1)
     gu_finish()
     for ch in range(n):
@@ -650,9 +758,11 @@
     width = rows.shape[2]
     tok = side.shape[1]
     pad = -(-NZ * cap // LANES) * LANES
-    quarter = width // 4
-    chunks = [([(0, 0, LANES, 0), (1, 0, quarter, LANES)], LANES + quarter)]
-    chunks += [([(1, k * quarter, quarter, 0)], quarter) for k in (1, 2, 3)]
+    chunks, col = [], 0
+    for w in BACK_CHUNKS:
+        off = 0 if chunks else LANES
+        chunks.append(([(0, 0, LANES, 0)] * (off > 0) + [(1, col, w, off)], off + w))
+        col += w
     n = len(chunks)
     vmem = pl.BlockSpec(memory_space=pltpu.VMEM)
     shape = jax.ShapeDtypeStruct
@@ -695,11 +805,10 @@
             zeros((LANES - GATE_LANE - top, tok_rows)),
         ]
     )
+    grad_scale = float(1.0 / (groups * tok_rows * top) ** 0.5)
     sides, x_rows, pre, gate_rows, rows, grad_dn = front(
-        side, out_grad, tokens, saved_preacts[0, 0], gate_up[0], down_proj[0], cap
+        side, out_grad, tokens, saved_preacts[0, 0], gate_up[0], down_proj[0], cap, grad_scale
     )
-    grad_scale = float(1.0 / (groups * tok_rows * top) ** 0.5)
-    grad_dn = lax.psum_scatter(grad_dn, "dp", scatter_dimension=0, tiled=True).astype(F32) * grad_scale
     gates, grad_tokens, grad_gu = back(sides, gate_rows, rows, x_rows, pre, cap, gate_up.shape[1], grad_scale)
     return (grad_tokens, gates[:, :top], grad_gu[None], grad_dn[None])
 

time: 238 us -> 220 us (0.924)
  between operations: 14.1 us -> 0.66 us
  Pallas kernels: 214 us -> 209 us
  local copies, waits for them, and re-layouts: 5.19 us -> 8.25 us
  other arithmetic: 4.47 us -> 2.09 us
    pallas_call x1, Pallas kernels: 88.9 us -> 85.6 us  [back(): pl.pallas_call(functools.partial(back_kernel, chunks, cap, scale), out_sh...]
    unnamed x5 -> x6, local copies, waits for them, and re-layouts: 5.03 us -> 8.09 us
    broadcast_in_dim x1 -> x0, other arithmetic: 2.38 us -> none  [on_device(): return (grad_tokens, gates[:, :top], grad_gu[None], grad_dn[None])]
  transfers between devices with their start and end apart: 1 -> 0, of which waited for: 0 -> 0; matrix products, arithmetic and copies ran while one was open for 1% -> 0% of each run, Pallas kernels for 37% -> 0%
where the time goes in v3:
time: 220 us
  Pallas kernels  209 us (95%)
  local copies, waits for them, and re-layouts  8.25 us (4%)
    pallas_call x1, Pallas kernels, front(): pl.pallas_call(functools.partial(front_kernel, chunks, cap, scale), out_s...  124 us
    pallas_call x1, Pallas kernels, back(): pl.pallas_call(functools.partial(back_kernel, chunks, cap, scale), out_sh...  85.6 us
    unnamed x6, local copies, waits for them, and re-layouts  8.09 us

profile of v3, /device:TPU:1, one launch (start us, length us, event | category | flops | bytes accessed | tf_op | source)
XLA Modules:
  0.0 220.1 jit_solution(16159665513322920619)
XLA Ops:
  0.6 0.1 pad.3.clone
  0.7 0.1 pad.1.clone
  0.8 0.7 convert_bitcast_fusion
  1.5 1.4 maximum_maximum_fusion.side_in
  2.9 123.5 %front.1 = (bf16[8,128,128]{2,1,0:T(8,128)(2,1)}, bf16[8,112,2048]{2,1,0:T(8,128)(2,1)}, bf16[896,1408]{1,0:T(8,128)(2,1)}, bf16[8,112,128]{2,1,0:T(8,128)(2,1)}...) custom-call(bf16[128,128]{1,0:T(8,128)(2,1)} %maximum_maximum_fusion.side_in, bf16[128,2048]{1,0:T(8,128)(2,1)} %dy_in.1, ...), custom_call_target="tpu_custom_call" | custom-call | flops 20000000000 | bytes 350000000 | tf_op jit(solution)/shard_map/front/pallas_call | solution.py:476
  126.4 85.6 %back.1 = (bf16[128,128]{1,0:T(8,128)(2,1)}, bf16[128,2048]{1,0:T(8,128)(2,1)}, f32[512,1408]{1,0:T(8,128)}) custom-call(bf16[8,128,128]{2,1,0:T(8,128)(2,1)} %get-tuple-element.13.side_ref, bf16[8,112,128]{2,1,0:T(8,128)(2,1)} %get-tuple-element.14.gate_ref, bf16[8,112,2048]{2,1,0:T(8,128)(2,1)} %get-tuple-element.15.row_ref, ...), custom_call_target="tpu_custom_call" | custom-call | flops 10000000000 | bytes 250000000 | tf_op jit(solution)/shard_map/back/pallas_call | solution.py:769
  212.0 1.4 copy.11
  213.5 1.9 copy.15
  215.3 0.0 copy-start
  215.3 3.7 %copy.16 = f32[1,512,1408]{2,1,0:T(8,128)} copy(f32[1,512,1408]{2,1,0:T(8,128)} %bitcast.9) | data formatting | bytes 5767168
  219.0 0.0 copy-done
  219.0 1.1 copy.17
  (2 shorter events, 0.0 us)
Async XLA Ops:
  215.3 3.7 %copy-start = (f32[176,2048]{1,0:T(8,128)S(1)}, f32[176,2048]{1,0:T(8,128)}, u32[]{:S(2)}) copy-start(f32[176,2048]{1,0:T(8,128)} %get-tuple-element.21) | copy-start | bytes 4325380

commit v4 on v3

--- a/solution.py
+++ b/solution.py
@@ -63,17 +63,17 @@
     down_in,
     side_out,
     x_out,
-    pre_out,
+    pre_hbm,
     gate_out,
-    row_out,
+    row_hbm,
     dn_out,
     *scratch,
 ):
     n = len(chunks)
     ring, stage = scratch[:n], scratch[n : n + n // 2] * 2
     later = scratch[n + n // 2 :]
-    side_own, side_rows, dy_rows, scaled_rows, pick, up, down, act, turned_act, coef_gate, coef_up, dn, dn_come, dn_sum = later[:14]
-    z_send, z_recv, x_send, x_recv, own_sem, y_send, y_recv, y_own, d_send, d_recv = later[14:]
+    side_own, side_rows, dy_rows, scaled_rows, pick, up, down, act, turned_act, coef_gate, coef_up, dn, dn_come, dn_sum, pre_out, row_out = later[:16]
+    z_send, z_recv, x_send, x_recv, own_sem, y_send, y_recv, y_own, d_send, d_recv, w_sem = later[16:]
     ins, outs = (side_own, dy_in, x_in), (side_rows, dy_rows, x_out)
     x, z, c = place()
     y = lax.axis_index("dp")
@@ -92,7 +92,7 @@
     for segments, buf in ((s, b) for (s, _), b in zip(chunks, ring)):
         for array, col, w, off in segments:
             buf[z, :, off : off + w] = ins[array][:, col : col + w]
-    for buf in outs:
+    for buf in outs[:2]:
         buf[:, block:, :] = jnp.zeros((PEERS, padded - block, buf.shape[2]), BF16)
     enter(x, z, c)
 
@@ -265,6 +265,14 @@
             part = dy_rows[two, :, at : at + 512].reshape(unit, 512).astype(F32)
             scaled_rows[two, :, at : at + 512] = (gain * part).astype(BF16).reshape(NC, padded, 512)
 
+    def pre_copy(b):
+        rows = aligned(b, unit)
+        return pltpu.make_async_copy(pre_out.at[rows, :], pre_hbm.at[rows, :], w_sem.at[0, b])
+
+    def row_copy(b):
+        two = pl.ds(b * NC, NC)
+        return pltpu.make_async_copy(row_out.at[two], row_hbm.at[two], w_sem.at[1, b])
+
     def through_down(b):
         rows = aligned(b, unit)
         two = pl.ds(b * NC, NC)
@@ -281,6 +289,7 @@
         scaled = gain * act_grad
         pre_out[rows, 0:hidden] = (scaled * coef_gate[rows, :]).astype(BF16)
         pre_out[rows, hidden : 2 * hidden] = (scaled * coef_up[rows, :]).astype(BF16)
+        pre_copy(b).start()
 
     def through_up(b):
         rows = aligned(b, unit)
@@ -292,6 +301,7 @@
             return 0
 
         lax.fori_loop(0, NY, one, 0)
+        row_copy(b).start()
 
     def down_grad(k):
         cols = aligned(k, 512)
@@ -448,6 +458,9 @@
             return 0
 
         lax.fori_loop(0, sends, drain, 0)
+    for b in range(NX):
+        pre_copy(b).wait()
+        row_copy(b).wait()
     for k in (0, 1):
         for h in range(6):
             y_copy(k, h).wait_send()
@@ -484,7 +497,7 @@
             shape((hidden // NY, width), F32),
         ),
         in_specs=[vmem] * 4 + [anywhere] * 2,
-        out_specs=(vmem,) * 6,
+        out_specs=(vmem, anywhere, anywhere, vmem, anywhere, vmem),
         scratch_shapes=[pltpu.VMEM((NZ, tok, w), BF16) for _, w in chunks]
         + [pltpu.VMEM((PEERS, block, max(a[1], b[1])), BF16) for a, b in zip(chunks[: n // 2], chunks[n // 2 :])]
         + [
@@ -502,6 +515,8 @@
             pltpu.VMEM((NY, hidden // NY, width), BF16),
             pltpu.VMEM((6, dn_part, width), BF16),
             pltpu.VMEM((2, dn_part, width), BF16),
+            pltpu.VMEM((rows, 2 * hidden), BF16),
+            pltpu.VMEM((PEERS, padded, width), BF16),
             pltpu.SemaphoreType.DMA((n, 2, NZ - 1)),
             pltpu.SemaphoreType.DMA((n, 2, NZ - 1)),
             pltpu.SemaphoreType.DMA((n, 2, PEERS)),
@@ -512,6 +527,7 @@
             pltpu.SemaphoreType.DMA((2,)),
             pltpu.SemaphoreType.DMA((6,)),
             pltpu.SemaphoreType.DMA((6,)),
+            pltpu.SemaphoreType.DMA((2, NX)),
         ],
         compiler_params=pltpu.CompilerParams(collective_id=0, has_side_effects=True, vmem_limit_bytes=62 << 20),
         cost_estimate=pl.CostEstimate(flops=20_000_000_000, bytes_accessed=350_000_000, transcendentals=0),
@@ -520,11 +536,11 @@
 
 
 def back_kernel(
-    chunks, cap, scale, side_ref, gate_ref, row_ref, x_ref, pre_ref, gate_out, tok_out, gu_out, *scratch
+    chunks, cap, scale, side_ref, gate_ref, row_ref, x_hbm, pre_hbm, gate_out, tok_out, gu_out, *scratch
 ):
     n = len(chunks)
     landed, total, leave, come = (scratch[k * n : (k + 1) * n] for k in range(4))
-    spread, gu_leave, gu_come, z_send, z_recv, x_send, x_recv, own_sem, y_send, y_recv = scratch[4 * n :]
+    spread, gu_leave, gu_come, x_ref, pre_ref, z_send, z_recv, x_send, x_recv, own_sem, y_send, y_recv, in_sem = scratch[4 * n :]
     ins, outs = (gate_ref, row_ref), (gate_out, tok_out)
     x, z, c = place()
     y = lax.axis_index("dp")
@@ -536,6 +552,13 @@
     pad = landed[0].shape[1]
     sends = NZ - 1
 
+    x_ref[:, block:, :] = jnp.zeros((PEERS, padded - block, x_ref.shape[2]), BF16)
+    fetches = (
+        pltpu.make_async_copy(x_hbm.at[:, 0:block, :], x_ref.at[:, 0:block, :], in_sem.at[0]),
+        pltpu.make_async_copy(pre_hbm, pre_ref, in_sem.at[1]),
+    )
+    for copy in fetches:
+        copy.start()
     for buf, (_, w) in zip(landed, chunks):
         buf[:, block:, :] = jnp.zeros((PEERS, pad - block, w), BF16)
     enter(x, z, c)
@@ -617,6 +640,8 @@
             gu_hop(b).wait_recv()
             gu_out[rows, :] = (gu_out[rows, :] + gu_come[a].astype(F32) + gu_come[b].astype(F32)) * scale
 
+    for copy in fetches:
+        copy.wait()
     gu_send(0)
     gu_send(3)
 
@@ -769,7 +794,7 @@
     return pl.pallas_call(
         functools.partial(back_kernel, chunks, cap, scale),
         out_shape=(shape((tok, LANES), BF16), shape((tok, width), BF16), shape((gu_rows, pre.shape[1]), F32)),
-        in_specs=[vmem] * 5,
+        in_specs=[vmem, vmem] + [pl.BlockSpec(memory_space=pl.ANY)] * 3,
         out_specs=(vmem,) * 3,
         scratch_shapes=[pltpu.VMEM((PEERS, pad, w), BF16) for _, w in chunks]
         + [pltpu.VMEM((NZ, tok, w), F32) for _, w in chunks]
@@ -778,6 +803,8 @@
             pltpu.VMEM((NZ, tok, PEERS * pad), BF16),
             pltpu.VMEM((6, gu_rows // 2, pre.shape[1]), BF16),
             pltpu.VMEM((6, gu_rows // 2, pre.shape[1]), BF16),
+            pltpu.VMEM(x_rows.shape, BF16),
+            pltpu.VMEM(pre.shape, BF16),
             pltpu.SemaphoreType.DMA((n, 2, NZ - 1)),
             pltpu.SemaphoreType.DMA((n, 2, NZ - 1)),
             pltpu.SemaphoreType.DMA((n, 2, PEERS)),
@@ -785,6 +812,7 @@
             pltpu.SemaphoreType.DMA((n, 2)),
             pltpu.SemaphoreType.DMA((6,)),
             pltpu.SemaphoreType.DMA((6,)),
+            pltpu.SemaphoreType.DMA((2,)),
         ],
         compiler_params=pltpu.CompilerParams(collective_id=1, has_side_effects=True, vmem_limit_bytes=62 << 20),
         cost_estimate=pl.CostEstimate(flops=10_000_000_000, bytes_accessed=250_000_000, transcendentals=0),

time: 220 us -> 215 us (0.977)
  Pallas kernels: 209 us -> 203 us
    pallas_call x1, Pallas kernels: 85.6 us -> 82.7 us  [back(): pl.pallas_call(functools.partial(back_kernel, chunks, cap, scale), out_sh...]
    pallas_call x1, Pallas kernels: 124 us -> 121 us  [front(): pl.pallas_call(functools.partial(front_kernel, chunks, cap, scale), out_s...]
where the time goes in v4:
time: 215 us; the launch traced here: 214 us
  Pallas kernels  203 us (94%)
  local copies, waits for them, and re-layouts  8.25 us (4%)
    pallas_call x1, Pallas kernels, front(): pl.pallas_call(functools.partial(front_kernel, chunks, cap, scale), out_s...  121 us
    pallas_call x1, Pallas kernels, back(): pl.pallas_call(functools.partial(back_kernel, chunks, cap, scale), out_sh...  82.7 us
    unnamed x6, local copies, waits for them, and re-layouts  8.09 us

profile of v4, /device:TPU:1, one launch (start us, length us, event | category | flops | bytes accessed | tf_op | source)
XLA Modules:
  0.0 214.4 jit_solution(5096061400904674254)
XLA Ops:
  0.6 0.1 pad.3.clone
  0.7 0.1 pad.1.clone
  0.8 0.7 convert_bitcast_fusion
  1.5 1.4 maximum_maximum_fusion.side_in
  2.9 120.6 %front.1 = (bf16[8,128,128]{2,1,0:T(8,128)(2,1)}, bf16[8,112,2048]{2,1,0:T(8,128)(2,1)}, bf16[896,1408]{1,0:T(8,128)(2,1)}, bf16[8,112,128]{2,1,0:T(8,128)(2,1)}...) custom-call(bf16[128,128]{1,0:T(8,128)(2,1)} %maximum_maximum_fusion.side_in, bf16[128,2048]{1,0:T(8,128)(2,1)} %dy_in.1, ...), custom_call_target="tpu_custom_call" | custom-call | flops 20000000000 | bytes 350000000 | tf_op jit(solution)/shard_map/front/pallas_call | solution.py:489
  123.5 82.7 %back.1 = (bf16[128,128]{1,0:T(8,128)(2,1)}, bf16[128,2048]{1,0:T(8,128)(2,1)}, f32[512,1408]{1,0:T(8,128)}) custom-call(bf16[8,128,128]{2,1,0:T(8,128)(2,1)} %get-tuple-element.13.side_ref, bf16[8,112,128]{2,1,0:T(8,128)(2,1)} %get-tuple-element.14.gate_ref, bf16[8,112,2048]{2,1,0:T(8,128)(2,1)} %get-tuple-element.15.row_ref, ...), custom_call_target="tpu_custom_call" | custom-call | flops 10000000000 | bytes 250000000 | tf_op jit(solution)/shard_map/back/pallas_call | solution.py:794
  206.3 1.4 copy.11
  207.7 1.9 copy.15
  209.6 0.0 copy-start
  209.6 3.7 %copy.16 = f32[1,512,1408]{2,1,0:T(8,128)} copy(f32[1,512,1408]{2,1,0:T(8,128)} %bitcast.9) | data formatting | bytes 5767168
  213.3 0.0 copy-done
  213.3 1.1 copy.17
  (2 shorter events, 0.0 us)
Async XLA Ops:
  209.6 3.7 %copy-start = (f32[176,2048]{1,0:T(8,128)S(1)}, f32[176,2048]{1,0:T(8,128)}, u32[]{:S(2)}) copy-start(f32[176,2048]{1,0:T(8,128)} %get-tuple-element.21) | copy-start | bytes 4325380

commit v5 on v4

--- a/solution.py
+++ b/solution.py
@@ -814,7 +814,7 @@
             pltpu.SemaphoreType.DMA((6,)),
             pltpu.SemaphoreType.DMA((2,)),
         ],
-        compiler_params=pltpu.CompilerParams(collective_id=1, has_side_effects=True, vmem_limit_bytes=62 << 20),
+        compiler_params=pltpu.CompilerParams(collective_id=1, has_side_effects=True, vmem_limit_bytes=47 << 20),
         cost_estimate=pl.CostEstimate(flops=10_000_000_000, bytes_accessed=250_000_000, transcendentals=0),
         name="back",
     )(side, gate_rows, rows, x_rows, pre)

time: 215 us -> 213 us (level)
    pallas_call x1, Pallas kernels: 82.7 us -> 80.1 us  [back(): pl.pallas_call(functools.partial(back_kernel, chunks, cap, scale), out_sh...]
    unnamed x6 -> x12, local copies, waits for them, and re-layouts: 8.09 us -> 8.55 us
where the time goes in v5:
time: 213 us; the launch traced here: 212 us
  Pallas kernels  201 us (94%)
  local copies, waits for them, and re-layouts  8.71 us (4%)
    pallas_call x1, Pallas kernels, front(): pl.pallas_call(functools.partial(front_kernel, chunks, cap, scale), out_s...  121 us
    pallas_call x1, Pallas kernels, back(): pl.pallas_call(functools.partial(back_kernel, chunks, cap, scale), out_sh...  80.1 us
    unnamed x12, local copies, waits for them, and re-layouts  8.55 us

profile of v5, /device:TPU:1, one launch (start us, length us, event | category | flops | bytes accessed | tf_op | source)
XLA Modules:
  0.0 212.2 jit_solution(4353227187658509960)
XLA Ops:
  0.6 0.1 pad.3.clone
  0.7 0.1 pad.1.clone
  0.8 0.7 convert_bitcast_fusion
  1.5 1.4 maximum_maximum_fusion.side_in
  2.9 120.6 %front.1 = (bf16[8,128,128]{2,1,0:T(8,128)(2,1)}, bf16[8,112,2048]{2,1,0:T(8,128)(2,1)}, bf16[896,1408]{1,0:T(8,128)(2,1)}, bf16[8,112,128]{2,1,0:T(8,128)(2,1)}...) custom-call(bf16[128,128]{1,0:T(8,128)(2,1)} %maximum_maximum_fusion.side_in, bf16[128,2048]{1,0:T(8,128)(2,1)} %dy_in.1, ...), custom_call_target="tpu_custom_call" | custom-call | flops 20000000000 | bytes 350000000 | tf_op jit(solution)/shard_map/front/pallas_call | solution.py:489
  123.5 0.0 copy-start
  123.5 1.7 copy-done
  125.2 0.0 copy-start.1
  125.2 0.9 copy-done.1
  126.1 0.0 copy-start.2
  126.1 0.9 copy-done.2
  127.1 80.1 %back.1 = (bf16[128,128]{1,0:T(8,128)(2,1)S(1)}, bf16[128,2048]{1,0:T(8,128)(2,1)S(1)}, f32[512,1408]{1,0:T(8,128)S(1)}) custom-call(bf16[8,128,128]{2,1,0:T(8,128)(2,1)S(1)} %copy-done.1, bf16[8,112,128]{2,1,0:T(8,128)(2,1)S(1)} %copy-done.2, bf16[8,112,2048]{2,1,0:T(8,128)(2,1)} %get-tuple-element.15.row_ref, ...), custom_call_target="tpu_custom_call" | custom-call | flops 10000000000 | bytes 250000000 | tf_op jit(solution)/shard_map/back/pallas_call | solution.py:794
  207.2 0.7 copy.11
  207.9 0.8 copy.15
  208.7 0.0 copy-start.3
  208.7 1.6 copy.16
  210.3 0.8 copy-done.3
  211.1 1.1 copy.17
  (2 shorter events, 0.0 us)
Async XLA Ops:
  123.5 1.7 copy-start
  125.2 0.9 copy-start.1
  126.1 0.9 copy-start.2
  208.7 2.4 %copy-start.3 = (f32[176,2048]{1,0:T(8,128)S(1)}, f32[176,2048]{1,0:T(8,128)}, u32[]{:S(2)}) copy-start(f32[176,2048]{1,0:T(8,128)} %get-tuple-element.21) | copy-start | bytes 4325380
